TPU v7x, 32 devices: a whole 2x2x4 slice. The times are simulated.
32 devices in a mesh: fsdp: 8 (over y, x, core), rep: 4 (over z).
Axes of the slice: x: 2, y: 2, z: 4, core: 2. Of those that a mesh axis runs over, the one named last changes fastest.
Arguments:
- tokens: bfloat16 [32, 1024, 1152], P(('fsdp', 'rep')), may hold values from -6 to 6
- condition: bfloat16 [32, 4, 1152], P(('fsdp', 'rep')), may hold values from -6 to 6
- heights: int32 [32, 4], P(('fsdp', 'rep')), may hold values from 8 to 16, as said below
- widths: int32 [32, 4], P(('fsdp', 'rep')), may hold values from 8 to 16, as said below
- lengths: int32 [32, 4], P(('fsdp', 'rep')), may hold values from 64 to 256, as said below
- segments: int32 [32, 1024], P(('fsdp', 'rep')), may hold values from 0 to 4, as said below
- ada_weight: float32 [1152, 6912], P('fsdp'), may hold values from -0.1875 to 0.1875
- ada_bias: float32 [6912], P('fsdp'), may hold values from -3 to 3
- qkv_weight: float32 [1152, 3456], P('fsdp'), may hold values from -0.1875 to 0.1875
- out_weight: float32 [1152, 1152], P('fsdp'), may hold values from -0.75 to 0.75
- gate_up_weight: float32 [1152, 6144], P('fsdp'), may hold values from -0.1875 to 0.1875
- down_weight: float32 [3072, 1152], P('fsdp'), may hold values from -0.109375 to 0.109375
- query_gain: float32 [72], replicated, may hold values from 1 to 2
- key_gain: float32 [72], replicated, may hold values from 1 to 2
- cotangent: bfloat16 [32, 1024, 1152], P(('fsdp', 'rep')), may hold values from -6 to 6
Outputs:
- out: bfloat16 [32, 1024, 1152], P(('fsdp', 'rep'))
- grad_tokens: bfloat16 [32, 1024, 1152], P(('fsdp', 'rep'))
- grad_condition: bfloat16 [32, 4, 1152], P(('fsdp', 'rep'))
- grad_ada_weight: float32 [1152, 6912], P('fsdp')
- grad_ada_bias: float32 [6912], P('fsdp')
- grad_qkv_weight: float32 [1152, 3456], P('fsdp')
- grad_out_weight: float32 [1152, 1152], P('fsdp')
- grad_gate_up_weight: float32 [1152, 6144], P('fsdp')
- grad_down_weight: float32 [3072, 1152], P('fsdp')
- grad_query_gain: float32 [72], replicated
- grad_key_gain: float32 [72], replicated
Inputs may be any that keep to these rules, and one draw needn't show every extreme that they name: `heights`: the first image of every sequence has 16 rows. `widths`: the first image of every sequence has 16 columns and the second half of 16. `lengths`: each length is that image's rows times its columns; the images of a sequence lie one after another from position 0 and leave padding at its end. `segments`: image i holds the positions given by lengths, in order; the positions after the last image are padding with number 4.
All inputs are finite; a program needn't handle non-finite values.
Results may differ from a plain program's by a relative error of at most 0.019.
The roundings to bfloat16 on the way count: a program that leaves them out, or rounds other values in their place, can miss the bound.
Values may be sent and summed in bfloat16 or wider, within the bound.
A program may use at most 320 MiB of HBM per device.

v0:
```python
import math

import jax
import jax.numpy as jnp
from jax import lax
from jax.sharding import PartitionSpec as P

D = 1152
HEADS = 16
HEAD_DIM = 72
FF = 3072
ITEMS = 4
GRID = 16
SEQ_LEN = 1024


epsilon = 1e-06
highest = lax.Precision.HIGHEST


def product(left, right):
    return jnp.dot(left, right, preferred_element_type=jnp.float32)


def left_product(left, right):
    return lax.dot_general(
        left, right, (((0,), (0,)), ((), ())), preferred_element_type=jnp.float32
    )


def right_product(left, right):
    return lax.dot_general(
        left, right, (((1,), (1,)), ((), ())), preferred_element_type=jnp.float32
    )


def grid_tables(heights_one, widths_one, lengths_one, segment_one):
    ends = jnp.cumsum(lengths_one)
    starts = ends - lengths_one
    places = jnp.arange(SEQ_LEN, dtype=jnp.int32)
    member = segment_one[:, None] == jnp.arange(ITEMS, dtype=jnp.int32)[None, :]
    start_tok = jnp.sum(jnp.where(member, starts[None, :], 0), axis=1)
    width_tok = jnp.sum(jnp.where(member, widths_one[None, :], 0), axis=1)
    height_tok = jnp.sum(jnp.where(member, heights_one[None, :], 0), axis=1)
    inside = width_tok > 0
    offset = places - start_tok
    safe_width = jnp.maximum(width_tok, 1)
    safe_height = jnp.maximum(height_tok, 1)
    row_index = jnp.where(inside, offset // safe_width, 0)
    col_index = jnp.where(inside, offset % safe_width, 0)
    height_f = safe_height.astype(jnp.float32)
    width_f = safe_width.astype(jnp.float32)
    row_place = jnp.where(
        inside, (row_index.astype(jnp.float32) - 0.5 * (height_f - 1.0)) * (GRID / height_f), 0.0
    )
    col_place = jnp.where(
        inside, (col_index.astype(jnp.float32) - 0.5 * (width_f - 1.0)) * (GRID / width_f), 0.0
    )
    quarter = HEAD_DIM // 4
    freqs = jnp.exp(jnp.arange(quarter, dtype=jnp.float32) * (-math.log(10000.0) / quarter))
    row_angle = row_place[:, None] * freqs[None, :]
    col_angle = col_place[:, None] * freqs[None, :]
    return (
        member.astype(jnp.float32),
        jnp.cos(row_angle),
        jnp.sin(row_angle),
        jnp.cos(col_angle),
        jnp.sin(col_angle),
    )


def rotate(values, tables, sign):
    quarter = values.shape[-1] // 4
    first = values[..., :quarter]
    second = values[..., quarter : 2 * quarter]
    third = values[..., 2 * quarter : 3 * quarter]
    fourth = values[..., 3 * quarter :]
    cos_row, sin_row, cos_col, sin_col = [t[..., None, :] for t in tables]
    return jnp.concatenate(
        [
            first * cos_row - sign * second * sin_row,
            second * cos_row + sign * first * sin_row,
            third * cos_col - sign * fourth * sin_col,
            fourth * cos_col + sign * third * sin_col,
        ],
        axis=-1,
    )


def rms_scale(values):
    return lax.rsqrt(jnp.mean(values * values, axis=-1, keepdims=True) + epsilon)


def rms_back(grad_normed, normed, factor):
    return factor * (grad_normed - normed * jnp.mean(grad_normed * normed, axis=-1, keepdims=True))


def per_device(
    tokens,
    condition,
    heights,
    widths,
    lengths,
    segments,
    ada_weight,
    ada_bias,
    qkv_weight,
    out_weight,
    gate_up_weight,
    down_weight,
    query_gain,
    key_gain,
    cotangent,
):
    seq_count = tokens.shape[0]
    length = tokens.shape[1]
    rows_all = seq_count * length
    items = condition.shape[1]
    quarter = HEAD_DIM // 4
    group_heads = 4
    groups = HEADS // group_heads
    block_rows = min(512, length)
    blocks = length // block_rows
    score_scale = HEAD_DIM ** (-0.5)
    member, cos_row, sin_row, cos_col, sin_col = jax.vmap(grid_tables)(
        heights, widths, lengths, segments
    )
    tables = tuple((t.reshape(rows_all, quarter) for t in (cos_row, sin_row, cos_col, sin_col)))
    mixing = (
        lax.all_gather(ada_weight.astype(jnp.bfloat16), "fsdp", axis=0, tiled=True),
        lax.all_gather(ada_bias.astype(jnp.bfloat16), "fsdp", axis=0, tiled=True),
        lax.all_gather(qkv_weight.astype(jnp.bfloat16), "fsdp", axis=0, tiled=True),
        lax.all_gather(out_weight.astype(jnp.bfloat16), "fsdp", axis=0, tiled=True),
    )
    feeding = (
        lax.all_gather(gate_up_weight.astype(jnp.bfloat16), "fsdp", axis=0, tiled=True),
        lax.all_gather(down_weight.astype(jnp.bfloat16), "fsdp", axis=0, tiled=True),
    )
    ada_full, bias_full, qkv_full, out_full = mixing
    gate_up_full, down_full = feeding
    cond_values = condition.astype(jnp.float32).reshape(seq_count * items, D)
    cond_act = jax.nn.silu(cond_values).astype(jnp.bfloat16)
    modulation = (product(cond_act, ada_full) + bias_full.astype(jnp.float32)).reshape(
        seq_count, items, 6 * D
    )

    def spread(which):
        return jnp.einsum(
            "sti,sid->std", member, modulation[:, :, which * D : (which + 1) * D], precision=highest
        ).reshape(rows_all, D)

    shift_a, scale_a, gate_a, shift_b, scale_b, gate_b = [spread(which) for which in range(6)]
    stream = tokens.reshape(rows_all, D).astype(jnp.float32)
    factor_a = rms_scale(stream)
    normed_a = stream * factor_a
    hidden_a = (normed_a * (1.0 + scale_a) + shift_a).astype(jnp.bfloat16)
    projected = product(hidden_a, qkv_full)
    query_raw = projected[:, :D].reshape(rows_all, HEADS, HEAD_DIM)
    key_raw = projected[:, D : 2 * D].reshape(rows_all, HEADS, HEAD_DIM)
    query_factor = rms_scale(query_raw)
    query_normed = query_raw * query_factor
    key_factor = rms_scale(key_raw)
    key_normed = key_raw * key_factor
    query = rotate(query_normed * query_gain, tables, 1.0).astype(jnp.bfloat16)
    keys = rotate(key_normed * key_gain, tables, 1.0).astype(jnp.bfloat16)
    values = projected[:, 2 * D :].astype(jnp.bfloat16).reshape(rows_all, HEADS, HEAD_DIM)

    def heads_first(array):
        return array.reshape(seq_count, length, HEADS, HEAD_DIM).transpose(0, 2, 1, 3)

    query_h = heads_first(query)
    key_h = heads_first(keys)
    value_h = heads_first(values)

    def take_block(array, seq, head, start, size):
        return lax.dynamic_slice(array, (seq, head, start, 0), (1, group_heads, size, HEAD_DIM))[0]

    def mask_scores(query_b, keys_b, seq, start):
        raw = (
            jnp.einsum("hqd,hkd->hqk", query_b, keys_b, preferred_element_type=jnp.float32)
            * score_scale
        )
        segment_q = lax.dynamic_slice(segments, (seq, start), (1, block_rows))[0]
        segment_k = lax.dynamic_index_in_dim(segments, seq, 0, keepdims=False)
        allowed = segment_q[:, None] == segment_k[None, :]
        return jnp.where(allowed[None], raw, -1000000000.0)

    def attend(position):
        seq = position // (groups * blocks)
        head = position // blocks % groups * group_heads
        start = position % blocks * block_rows
        scores = mask_scores(
            take_block(query_h, seq, head, start, block_rows),
            take_block(key_h, seq, head, 0, length),
            seq,
            start,
        )
        row_max = jnp.max(scores, axis=-1, keepdims=True)
        raised = jnp.exp(scores - row_max)
        row_total = jnp.sum(raised, axis=-1, keepdims=True)
        chance = raised / row_total
        result = jnp.einsum(
            "hqk,hkd->hqd",
            chance.astype(jnp.bfloat16),
            take_block(value_h, seq, head, 0, length),
            preferred_element_type=jnp.float32,
        )
        return (result, (row_max + jnp.log(row_total))[..., 0])

    attended, log_total = lax.map(attend, jnp.arange(seq_count * groups * blocks, dtype=jnp.int32))
    attended = attended.reshape(seq_count, groups, blocks, group_heads, block_rows, HEAD_DIM)
    attended_low = attended.transpose(0, 2, 4, 1, 3, 5).reshape(rows_all, D).astype(jnp.bfloat16)
    branch_a = product(attended_low, out_full)
    stream_b = stream + gate_a * branch_a
    factor_b = rms_scale(stream_b)
    normed_b = stream_b * factor_b
    hidden_b = (normed_b * (1.0 + scale_b) + shift_b).astype(jnp.bfloat16)
    gate_up = product(hidden_b, gate_up_full)
    gate_val = gate_up[:, :FF]
    up_val = gate_up[:, FF:]
    sigmoid_g = jax.nn.sigmoid(gate_val)
    inner = (gate_val * sigmoid_g * up_val).astype(jnp.bfloat16)
    branch_b = product(inner, down_full)
    result_tokens = (stream_b + gate_b * branch_b).astype(jnp.bfloat16).reshape(tokens.shape)
    mixing_again = (
        lax.all_gather(ada_weight.astype(jnp.bfloat16), "fsdp", axis=0, tiled=True),
        lax.all_gather(qkv_weight.astype(jnp.bfloat16), "fsdp", axis=0, tiled=True),
        lax.all_gather(out_weight.astype(jnp.bfloat16), "fsdp", axis=0, tiled=True),
    )
    feeding_again = (
        lax.all_gather(gate_up_weight.astype(jnp.bfloat16), "fsdp", axis=0, tiled=True),
        lax.all_gather(down_weight.astype(jnp.bfloat16), "fsdp", axis=0, tiled=True),
    )
    ada_back, qkv_back, out_back = mixing_again
    gate_up_back, down_back = feeding_again
    upstream = cotangent.reshape(rows_all, D).astype(jnp.float32)
    grad_gate_b = upstream * branch_b
    grad_branch_b = (upstream * gate_b).astype(jnp.bfloat16)
    grad_inner = right_product(grad_branch_b, down_back)
    grad_down = left_product(inner, grad_branch_b)
    grad_gate_val = grad_inner * up_val * sigmoid_g * (1.0 + gate_val * (1.0 - sigmoid_g))
    grad_up_val = grad_inner * gate_val * sigmoid_g
    grad_gate_up_act = jnp.concatenate([grad_gate_val, grad_up_val], axis=1).astype(jnp.bfloat16)
    grad_gate_up = left_product(hidden_b, grad_gate_up_act)
    grad_hidden_b = right_product(grad_gate_up_act, gate_up_back)
    grad_scale_b = grad_hidden_b * normed_b
    grad_stream_b = upstream + rms_back(grad_hidden_b * (1.0 + scale_b), normed_b, factor_b)
    grad_gate_a = grad_stream_b * branch_a
    grad_branch_a = (grad_stream_b * gate_a).astype(jnp.bfloat16)
    grad_out = left_product(attended_low, grad_branch_a)
    grad_attended = right_product(grad_branch_a, out_back).astype(jnp.bfloat16)
    grad_h = heads_first(grad_attended)
    log_blocks = log_total.reshape(seq_count * groups, blocks, group_heads, block_rows)

    def attend_back(position):
        seq = position // groups
        head = position % groups * group_heads
        keys_b = take_block(key_h, seq, head, 0, length)
        values_b = take_block(value_h, seq, head, 0, length)
        logs = lax.dynamic_index_in_dim(log_blocks, position, 0, keepdims=False)

        def one_block(carry, block):
            grad_keys, grad_values = carry
            start = block * block_rows
            query_b = take_block(query_h, seq, head, start, block_rows)
            grad_result = take_block(grad_h, seq, head, start, block_rows)
            scores = mask_scores(query_b, keys_b, seq, start)
            chance = jnp.exp(
                scores - lax.dynamic_index_in_dim(logs, block, 0, keepdims=False)[..., None]
            )
            grad_chance = jnp.einsum(
                "hqd,hkd->hqk", grad_result, values_b, preferred_element_type=jnp.float32
            )
            delta = jnp.sum(chance * grad_chance, axis=-1, keepdims=True)
            grad_scores = (chance * (grad_chance - delta)).astype(jnp.bfloat16)
            grad_query_b = (
                jnp.einsum("hqk,hkd->hqd", grad_scores, keys_b, preferred_element_type=jnp.float32)
                * score_scale
            )
            grad_keys = (
                grad_keys
                + jnp.einsum(
                    "hqk,hqd->hkd", grad_scores, query_b, preferred_element_type=jnp.float32
                )
                * score_scale
            )
            grad_values = grad_values + jnp.einsum(
                "hqk,hqd->hkd",
                chance.astype(jnp.bfloat16),
                grad_result,
                preferred_element_type=jnp.float32,
            )
            return ((grad_keys, grad_values), grad_query_b)

        empty = jnp.zeros((group_heads, length, HEAD_DIM), jnp.float32)
        (grad_keys, grad_values), grad_queries = lax.scan(
            one_block, (empty, empty), jnp.arange(blocks, dtype=jnp.int32)
        )
        return (grad_queries, grad_keys, grad_values)

    grad_q_blocks, grad_k_groups, grad_v_groups = lax.map(
        attend_back, jnp.arange(seq_count * groups, dtype=jnp.int32)
    )
    grad_query = grad_q_blocks.reshape(seq_count, groups, blocks, group_heads, block_rows, HEAD_DIM)
    grad_query = grad_query.transpose(0, 2, 4, 1, 3, 5).reshape(rows_all, HEADS, HEAD_DIM)
    grad_key = grad_k_groups.reshape(seq_count, groups, group_heads, length, HEAD_DIM)
    grad_key = grad_key.transpose(0, 3, 1, 2, 4).reshape(rows_all, HEADS, HEAD_DIM)
    grad_value = grad_v_groups.reshape(seq_count, groups, group_heads, length, HEAD_DIM)
    grad_value = grad_value.transpose(0, 3, 1, 2, 4).reshape(rows_all, D)
    grad_query_rot = rotate(grad_query, tables, -1.0)
    grad_key_rot = rotate(grad_key, tables, -1.0)
    query_gain_part = jnp.sum(grad_query_rot * query_normed, axis=(0, 1))
    key_gain_part = jnp.sum(grad_key_rot * key_normed, axis=(0, 1))
    grad_query_raw = rms_back(grad_query_rot * query_gain, query_normed, query_factor).reshape(
        rows_all, D
    )
    grad_key_raw = rms_back(grad_key_rot * key_gain, key_normed, key_factor).reshape(rows_all, D)
    grad_projected = jnp.concatenate([grad_query_raw, grad_key_raw, grad_value], axis=1).astype(
        jnp.bfloat16
    )
    grad_qkv = left_product(hidden_a, grad_projected)
    grad_hidden_a = right_product(grad_projected, qkv_back)
    stream_grad = grad_stream_b + rms_back(grad_hidden_a * (1.0 + scale_a), normed_a, factor_a)

    def collect(piece):
        return jnp.einsum(
            "sti,std->sid", member, piece.reshape(seq_count, length, D), precision=highest
        )

    pieces = (
        grad_hidden_a,
        grad_hidden_a * normed_a,
        grad_gate_a,
        grad_hidden_b,
        grad_scale_b,
        grad_gate_b,
    )
    grad_mod = jnp.concatenate([collect(piece) for piece in pieces], axis=2)
    grad_mod = grad_mod.reshape(seq_count * items, 6 * D).astype(jnp.bfloat16)
    grad_bias = jnp.sum(grad_mod.astype(jnp.float32), axis=0)
    grad_cond_act = right_product(grad_mod, ada_back)
    sigmoid_c = jax.nn.sigmoid(cond_values)
    grad_condition = (grad_cond_act * sigmoid_c * (1.0 + cond_values * (1.0 - sigmoid_c))).astype(
        jnp.bfloat16
    )
    grad_ada = lax.psum_scatter(
        left_product(cond_act, grad_mod).astype(jnp.bfloat16),
        "fsdp",
        scatter_dimension=0,
        tiled=True,
    )
    sharded = (
        lax.psum_scatter(
            grad_bias.astype(jnp.bfloat16), "fsdp", scatter_dimension=0, tiled=True
        ).astype(jnp.float32),
        lax.psum_scatter(
            grad_qkv.astype(jnp.bfloat16), "fsdp", scatter_dimension=0, tiled=True
        ).astype(jnp.float32),
        lax.psum_scatter(
            grad_out.astype(jnp.bfloat16), "fsdp", scatter_dimension=0, tiled=True
        ).astype(jnp.float32),
        lax.psum_scatter(
            grad_gate_up.astype(jnp.bfloat16), "fsdp", scatter_dimension=0, tiled=True
        ).astype(jnp.float32),
        lax.psum_scatter(
            grad_down.astype(jnp.bfloat16), "fsdp", scatter_dimension=0, tiled=True
        ).astype(jnp.float32),
    )
    totals = (
        lax.psum(grad_ada, "rep").astype(jnp.float32),
        lax.psum(sharded[0].astype(jnp.bfloat16), "rep").astype(jnp.float32),
        lax.psum(sharded[1].astype(jnp.bfloat16), "rep").astype(jnp.float32),
        lax.psum(sharded[2].astype(jnp.bfloat16), "rep").astype(jnp.float32),
        lax.psum(sharded[3].astype(jnp.bfloat16), "rep").astype(jnp.float32),
        lax.psum(sharded[4].astype(jnp.bfloat16), "rep").astype(jnp.float32),
    )
    gains = lax.psum((query_gain_part, key_gain_part), ("fsdp", "rep"))
    return (
        result_tokens,
        stream_grad.astype(jnp.bfloat16).reshape(tokens.shape),
        grad_condition.reshape(condition.shape),
        totals[0],
        totals[1],
        totals[2],
        totals[3],
        totals[4],
        totals[5],
        gains[0],
        gains[1],
    )


def solution(mesh):
    return jax.shard_map(
        per_device,
        mesh=mesh,
        in_specs=(
            P(("fsdp", "rep"), None, None),
            P(("fsdp", "rep"), None, None),
            P(("fsdp", "rep"), None),
            P(("fsdp", "rep"), None),
            P(("fsdp", "rep"), None),
            P(("fsdp", "rep"), None),
            P("fsdp", None),
            P("fsdp"),
            P("fsdp", None),
            P("fsdp", None),
            P("fsdp", None),
            P("fsdp", None),
            P(),
            P(),
            P(("fsdp", "rep"), None, None),
        ),
        out_specs=(
            P(("fsdp", "rep"), None, None),
            P(("fsdp", "rep"), None, None),
            P(("fsdp", "rep"), None, None),
            P("fsdp", None),
            P("fsdp"),
            P("fsdp", None),
            P("fsdp", None),
            P("fsdp", None),
            P("fsdp", None),
            P(),
            P(),
        ),
        check_vma=False,
    )
```

profile of v0, /device:TPU:0, one launch (start us, length us, event | category | flops | bytes accessed | tf_op | source)
XLA Modules:
  0.0 1429.6 jit_solution(1705408152864134366)
XLA Ops:
  20.9 27.3 %all-reduce = bf16[6912]{0:T(1024)(128)(2,1)S(1)} all-reduce(bf16[6912]{0:T(1024)(128)(2,1)S(1)} %dynamic-update-slice), channel_id=1, replica_groups=mesh['fsdp'=8,'rep'=4] {'fsdp'}, use_global_device_ids=true, to_apply=%add | all-reduce | flops 6912 | bytes 27648
  50.7 49.6 %all-gather.6.cloned.1.call-done = bf16[1152,6912]{1,0:T(8,128)(2,1)} async-done(((bf16[144,6912]{1,0:T(8,128)(2,1)}), bf16[1152,6912]{1,0:T(8,128)(2,1)}) %all-gather.6.cloned.1.call-update) | async-done | bytes 15925264 | tf_op jit(solution)/shard_map/all_gather | solution.py:130
  100.3 7.7 fusion.43
  117.0 38.2 %all-gather.8.cloned.1.call-done = bf16[1152,3456]{1,0:T(8,128)(2,1)} async-done(((bf16[144,3456]{1,0:T(8,128)(2,1)}), bf16[1152,3456]{1,0:T(8,128)(2,1)}) %all-gather.8.cloned.1.call-update) | async-done | bytes 7962640 | tf_op jit(solution)/shard_map/all_gather | solution.py:132
  155.2 13.3 fusion.153
  176.5 6.2 copy.72
  185.9 6.1 copy.71
  212.5 120.0 %while.62 = (s32[]{:T(128)}, bf16[8,4,512,72]{2,3,1,0:T(8,128)(2,1)}, f32[8,4,512]{2,1,0:T(4,128)}, s32[8]{0:T(128)S(1)}, s32[1,1024]{1,0:T(1,128)S(1)}, /*index...) while((s32[]{:T(128)}, ...), condition=%wide.region_10.11_spmd, body=%wide.region_7.10_spmd.sunk | while | flops 629667840 | bytes 29406260 | solution.py:210
  339.5 6.2 fusion.154
  360.7 23.4 %fusion.155 = f32[1024,6144]{1,0:T(8,128)} fusion(bf16[1024,1152]{1,0:T(8,128)(2,1)S(1)} %fusion.64, bf16[1152,6144]{1,0:T(8,128)(2,1)} %all-gather.12.cloned.1.call-done), kind=kOutput, calls=%fused_computation.265 | convolution fusion | flops 14495514624 | bytes 41680896 | tf_op jit(solution)/shard_map/dot_general | solution.py:22
  384.0 27.9 %multiply_convert_fusion.2 = (bf16[1024,3072]{1,0:T(8,128)(2,1)}, bf16[1024,3072]{1,0:T(8,128)(2,1)}, bf16[1024,3072]{1,0:T(8,128)(2,1)}) fusion(f32[1024,6144]{1,0:T(8,128)} %fusion.155, bf16[3072,1152]{1,0:T(8,128)(2,1)} %all-gather.14.cloned.1.call-done, f32[1024,1152]{1,0:T(8,128)} %fusion.111, bf16[1,1024,1152]{2,1,0:T(8,128)(2,1)} %param.35), kind=kOutput, calls=%fused_computation.64 | convolution fusion | flops 7301627904 | bytes 58195968 | tf_op jit(solution)/shard_map/dot_general | solution.py:32
  412.0 28.9 %multiply_reduce_fusion.5 = (f32[1024]{0:T(1024)S(1)}, f32[1024,1152]{1,0:T(8,128)}, f32[1024,1152]{1,0:T(8,128)}) fusion(f32[1024,1152]{1,0:T(8,128)} %copy-done.2, f32[1024]{0:T(1024)S(1)} %add_rsqrt_fusion.2, f32[1024,1152]{1,0:T(8,128)} %copy-done.14, bf16[1152,6144]{1,0:T(8,128)(2,1)} %all-gather.12.cloned.1.call-done, ...), kind=kOutput, calls=%fused_computation.110 | convolution fusion | flops 14525398016 | bytes 45621248 | tf_op jit(solution)/shard_map/dot_general | solution.py:32
  440.9 11.6 fusion.156
  452.6 8.4 multiply_convert_fusion.6
  462.4 6.4 convolution_convert_fusion.4
  470.4 7.6 convolution_convert_fusion.5
  482.3 13.7 convolution_convert_fusion.3
  496.7 299.9 %while.64 = (s32[]{:T(128)}, f32[4,2,4,512,72]{3,4,2,1,0:T(8,128)}, f32[4,4,1024,72]{2,3,1,0:T(8,128)}, bf16[4,4,1024,72]{2,3,1,0:T(8,128)(2,1)}, s32[4]{0:T(128...) while((s32[]{:T(128)}, f32[4,2,4,512,72]{3,4,2,1,0:T(8,128)}, ...), condition=%wide.region_17.18_spmd, body=%wide.region_13.17_spmd.sunk | while | flops 1543550976 | bytes 138909680 | solution.py:301
  503.7 65.8 %while.65 = (s32[]{:T(128)}, f32[4,1024,72]{1,2,0:T(8,128)S(1)}, f32[4,1024,72]{1,2,0:T(8,128)}, f32[2,4,512,72]{2,3,1,0:T(8,128)}, s32[2]{0:T(128)S(1)}, /*inde...) while((s32[]{:T(128)}, f32[4,1024,72]{1,2,0:T(8,128)S(1)}, ...), condition=%wide.region_16.16_spmd.clone, body=%wide.region_14.15_spmd.clone.sunk | while | flops 1543550976 | bytes 124719528 | solution.py:296
  530.3 6.9 fusion.217
  562.4 7.1 fusion.217
  580.2 63.6 %while.65 = (s32[]{:T(128)}, f32[4,1024,72]{1,2,0:T(8,128)S(1)}, f32[4,1024,72]{1,2,0:T(8,128)}, f32[2,4,512,72]{2,3,1,0:T(8,128)}, s32[2]{0:T(128)S(1)}, /*inde...) while((s32[]{:T(128)}, f32[4,1024,72]{1,2,0:T(8,128)S(1)}, ...), condition=%wide.region_16.16_spmd.clone, body=%wide.region_14.15_spmd.clone.sunk | while | flops 1543550976 | bytes 124719528 | solution.py:296
  605.0 6.8 fusion.217
  636.7 7.1 fusion.217
  654.5 63.6 %while.65 = (s32[]{:T(128)}, f32[4,1024,72]{1,2,0:T(8,128)S(1)}, f32[4,1024,72]{1,2,0:T(8,128)}, f32[2,4,512,72]{2,3,1,0:T(8,128)}, s32[2]{0:T(128)S(1)}, /*inde...) while((s32[]{:T(128)}, f32[4,1024,72]{1,2,0:T(8,128)S(1)}, ...), condition=%wide.region_16.16_spmd.clone, body=%wide.region_14.15_spmd.clone.sunk | while | flops 1543550976 | bytes 124719528 | solution.py:296
  679.3 6.7 fusion.217
  710.9 7.1 fusion.217
  728.7 63.5 %while.65 = (s32[]{:T(128)}, f32[4,1024,72]{1,2,0:T(8,128)S(1)}, f32[4,1024,72]{1,2,0:T(8,128)}, f32[2,4,512,72]{2,3,1,0:T(8,128)}, s32[2]{0:T(128)S(1)}, /*inde...) while((s32[]{:T(128)}, f32[4,1024,72]{1,2,0:T(8,128)S(1)}, ...), condition=%wide.region_16.16_spmd.clone, body=%wide.region_14.15_spmd.clone.sunk | while | flops 1543550976 | bytes 124719528 | solution.py:296
  753.5 6.7 fusion.217
  785.1 7.1 fusion.217
  796.5 8.1 copy.76
  804.7 7.4 reshape.1131
  828.5 6.1 copy.77
  844.9 6.1 copy.83
  851.1 6.2 copy.81
  860.1 6.2 copy.80
  878.2 13.9 multiply_reduce_fusion.1
  894.4 12.0 convolution_convert_fusion.2
  908.0 22.8 %convolution_convert_fusion.1 = bf16[1152,6144]{1,0:T(8,128)(2,1)} fusion(bf16[1024,1152]{1,0:T(8,128)(2,1)S(1)} %copy-done.32, bf16[1024,3072]{1,0:T(8,128)(2,1)} %get-tuple-element.634, bf16[1024,3072]{1,0:T(8,128)(2,1)} %get-tuple-element.633), kind=kOutput, calls=%fused_computation.60 | convolution fusion | flops 14527758336 | bytes 29097984 | tf_op jit(solution)/shard_map/dot_general | solution.py:26
  932.8 17.4 %fusion.48 = (f32[1024]{0:T(1024)S(1)}, f32[1024,1152]{1,0:T(8,128)}, f32[1024,1152]{1,0:T(8,128)}) fusion(bf16[1,1024,1152]{2,1,0:T(8,128)(2,1)S(1)} %copy-done.6, f32[1024]{0:T(1024)S(1)} %copy-done.50, f32[1024,1152]{1,0:T(8,128)} %copy-done.13, bf16[1152,3456]{1,0:T(8,128)(2,1)} %all-gather.8.cloned.1.call-done, bf16[1024,1152]{1,0:T(8,128)(2,1)} %copy-done.29, ...), kind=kOutput, calls=%fused_computation.87 | convolution fusion | flops 8180857856 | bytes 31563776 | tf_op jit(solution)/shard_map/dot_general | solution.py:32
  968.6 8.2 convolution_convert_fusion
  977.0 104.3 %reduce-scatter.12.cloned.1.call-done = bf16[144,6144]{1,0:T(8,128)(2,1)} async-done(((bf16[1152,6144]{1,0:T(8,128)(2,1)}), bf16[144,6144]{1,0:T(8,128)(2,1)}) %reduce-scatter.12.cloned.1.call-update) | async-done | bytes 1769488 | tf_op jit(solution)/shard_map/reduce_scatter | solution.py:362
  1081.3 114.7 %reduce-scatter.6.cloned.1.call-done = bf16[144,6912]{1,0:T(8,128)(2,1)} async-done(((bf16[1152,6912]{1,0:T(8,128)(2,1)}), bf16[144,6912]{1,0:T(8,128)(2,1)}) %reduce-scatter.6.cloned.1.call-update) | async-done | bytes 1990672 | tf_op jit(solution)/shard_map/reduce_scatter | solution.py:346
  1196.9 23.7 %all-reduce.1 = bf16[6912]{0:T(1024)(128)(2,1)S(1)} all-reduce(bf16[6912]{0:T(1024)(128)(2,1)S(1)} %reduce_sum.179), channel_id=3, replica_groups=mesh['fsdp'=8,'rep'=4] {'fsdp'}, use_global_device_ids=true, to_apply=%region_24.25.clone | all-reduce | flops 6912 | bytes 27648
  1220.7 14.3 %psum.57 = bf16[864]{0:T(1024)(128)(2,1)S(1)} all-reduce(bf16[864]{0:T(1024)(128)(2,1)S(1)} %dynamic-slice.2), channel_id=1, replica_groups=mesh['fsdp'=8,'rep'=4] {'rep'}, use_global_device_ids=true, to_apply=%region_25.26 | all-reduce | flops 864 | bytes 3456 | tf_op jit(solution)/shard_map/psum | solution.py:371
  1235.6 41.7 %all-reduce.2 = (f32[72]{0:T(128)}, f32[72]{0:T(128)}) all-reduce(f32[72]{0:T(128)S(1)} %reduce_sum.182, f32[72]{0:T(128)S(1)} %reduce_sum.185), channel_id=1, replica_groups=mesh['fsdp'=8,'rep'=4] {'fsdp','rep'}, use_global_device_ids=true, to_apply=%region_36.37 | all-reduce | flops 144 | bytes 1152 | tf_op jit(solution)/shard_map/psum | solution.py:377
  1277.3 10.4 fusion.84
  1293.1 119.8 %all-reduce.6.cloned.1.call-done = (bf16[144,6912]{1,0:T(8,128)(2,1)}, bf16[144,3456]{1,0:T(8,128)(2,1)}, bf16[144,1152]{1,0:T(8,128)(2,1)}, bf16[144,6144]{1,0:T(8,128)(2,1)}, bf16[384,1152]{1,0:T(8,128)(2,1)}) async-done(((bf16[144,6912]{1,0:T(8,128)(2,1)}, bf16[144,3456]{1,0:T(8,128)(2,1)}, bf16[144,1152]{1,0:T(8,128)(2,1)}, bf16[144,6144]{1,0:T(8,128)(2,1)}, bf16[384,1152]{1,0:T(8,128)(2,1)}), ...) | async-done | bytes 5971984 | tf_op jit(solution)/shard_map/psum | solution.py:370
  (542 shorter events, 469.0 us)
Async XLA Ops:
  7.2 93.1 %all-gather.6.cloned.1.call-start = ((), (), s32[]{:S(2)}) async-start(), calls=%async_computation.5 | async-start | bytes 17915904 | tf_op jit(solution)/shard_map/all_gather | solution.py:130
  11.0 144.2 %all-gather.8.cloned.1.call-start = ((), (), s32[]{:S(2)}) async-start(), calls=%async_computation.6 | async-start | bytes 8957952 | tf_op jit(solution)/shard_map/all_gather | solution.py:132
  12.2 327.4 %all-gather.10.cloned.1.call-start = ((), (), s32[]{:S(2)}) async-start(), calls=%async_computation.7 | async-start | bytes 2985984 | tf_op jit(solution)/shard_map/all_gather | solution.py:133
  13.0 6.4 copy-start.62
  13.0 35.2 %copy-start.4 = (bf16[1,1024,1152]{2,1,0:T(8,128)(2,1)S(1)}, bf16[1,1024,1152]{2,1,0:T(8,128)(2,1)}, u32[]{:S(2)}) copy-start(bf16[1,1024,1152]{2,1,0:T(8,128)(2,1)} %param.21) | copy-start | bytes 7077892
  13.1 347.6 %all-gather.12.cloned.1.call-start = ((), (), s32[]{:S(2)}) async-start(), calls=%async_computation.8 | async-start | bytes 15925248 | tf_op jit(solution)/shard_map/all_gather | solution.py:136
  16.7 32.1 %copy-start.65 = (s32[1,4]{1,0:T(1,128)S(1)}, s32[1,4]{1,0:T(1,128)}, u32[]{:S(2)}) copy-start(s32[1,4]{1,0:T(1,128)} %param.25) | copy-start | bytes 52
  16.7 32.3 %copy-start.16 = (s32[1,1024]{1,0:T(1,128)S(1)}, s32[1,1024]{1,0:T(1,128)}, u32[]{:S(2)}) copy-start(s32[1,1024]{1,0:T(1,128)} %param.26) | copy-start | bytes 12292
  16.7 32.3 %copy-start.63 = (s32[1,4]{1,0:T(1,128)S(1)}, s32[1,4]{1,0:T(1,128)}, u32[]{:S(2)}) copy-start(s32[1,4]{1,0:T(1,128)} %param.23) | copy-start | bytes 52
  16.7 32.3 %copy-start.64 = (s32[1,4]{1,0:T(1,128)S(1)}, s32[1,4]{1,0:T(1,128)}, u32[]{:S(2)}) copy-start(s32[1,4]{1,0:T(1,128)} %param.24) | copy-start | bytes 52
  16.7 83.6 %copy-start.47 = (bf16[1,4,1152]{2,1,0:T(4,128)(2,1)S(1)}, bf16[1,4,1152]{2,1,0:T(4,128)(2,1)}, u32[]{:S(2)}) copy-start(bf16[1,4,1152]{2,1,0:T(4,128)(2,1)} %param.22) | copy-start | bytes 27652
  16.7 367.3 %all-gather.14.cloned.1.call-start = ((), (), s32[]{:S(2)}) async-start(), calls=%async_computation.9 | async-start | bytes 7962624 | tf_op jit(solution)/shard_map/all_gather | solution.py:137
  19.3 957.6 %reduce-scatter.10.cloned.1.call-start = ((), (), s32[]{:S(2)}) async-start(), calls=%async_computation.12 | async-start | bytes 2985984 | tf_op jit(solution)/shard_map/reduce_scatter | solution.py:359
  48.8 61.6 %copy-start.49 = (f32[1024]{0:T(1024)}, f32[1024]{0:T(1024)S(1)}, u32[]{:S(2)}) copy-start(f32[1024]{0:T(1024)S(1)} %add_rsqrt_fusion.3) | copy-start | bytes 12292
  50.7 150.9 %copy-start.22 = (f32[1024,18]{0,1:T(8,128)}, f32[1024,18]{0,1:T(8,128)S(1)}, u32[]{:S(2)}) copy-start(f32[1024,18]{0,1:T(8,128)S(1)} %get-tuple-element.669) | copy-start | bytes 221188
  50.7 150.9 %copy-start.24 = (f32[1024,18]{0,1:T(8,128)}, f32[1024,18]{0,1:T(8,128)S(1)}, u32[]{:S(2)}) copy-start(f32[1024,18]{0,1:T(8,128)S(1)} %get-tuple-element.676) | copy-start | bytes 221188
  108.0 9.0 copy-start.44
  168.5 7.8 copy-start.7
  185.9 9.4 copy-start.35
  332.5 7.0 copy-start.1
  350.7 7.1 copy-start.2
  350.7 101.8 %copy-start.51 = (f32[1024]{0:T(1024)}, f32[1024]{0:T(1024)S(1)}, u32[]{:S(2)}) copy-start(f32[1024]{0:T(1024)S(1)} %add_rsqrt_fusion.2) | copy-start | bytes 12292
  360.6 23.4 %copy-start.31 = (bf16[1024,1152]{1,0:T(8,128)(2,1)}, bf16[1024,1152]{1,0:T(8,128)(2,1)S(1)}, u32[]{:S(2)}) copy-start(bf16[1024,1152]{1,0:T(8,128)(2,1)S(1)} %fusion.64) | copy-start | bytes 7077892
  384.0 68.5 %slice-start.2 = ((s8[4718592]{0:T(1024)(128)(4,1)}), s8[524288]{0:T(1024)(128)(4,1)S(1)}, s32[]{:S(2)}) async-start(s8[4718592]{0:T(1024)(128)(4,1)} %bitcast.321), calls=%async_computation.18 | async-start | bytes 1048576
  412.0 40.6 %slice-start.3 = ((s8[4718592]{0:T(1024)(128)(4,1)}), s8[4194304]{0:T(1024)(128)(4,1)S(1)}, s32[]{:S(2)}) async-start(s8[4718592]{0:T(1024)(128)(4,1)} %bitcast.321), calls=%async_computation.19 | async-start | bytes 8388608
  440.9 11.7 copy-start.18
  440.9 11.7 copy-start.21
  452.5 8.5 copy-start.11
  462.4 6.5 copy-start.56
  462.4 7.2 copy-start.59
  468.9 508.0 %reduce-scatter.14.cloned.1.call-start = ((), (), s32[]{:S(2)}) async-start(), calls=%async_computation.14 | async-start | bytes 7962624 | tf_op jit(solution)/shard_map/reduce_scatter | solution.py:365
  470.4 11.9 copy-start.19
  496.0 481.0 %reduce-scatter.8.cloned.1.call-start = ((), (), s32[]{:S(2)}) async-start(), calls=%async_computation.11 | async-start | bytes 8957952 | tf_op jit(solution)/shard_map/reduce_scatter | solution.py:356
  804.6 7.5 copy-start.23
  804.6 7.5 copy-start.25
  804.6 7.5 copy-start.40
  804.6 7.5 copy-start.41
  804.6 11.9 slice-start.10
  828.5 10.6 slice-start.6
  878.2 14.0 copy-start.29
  878.2 16.1 %copy-start.30 = (bf16[1024,1152]{1,0:T(8,128)(2,1)S(1)}, bf16[1024,1152]{1,0:T(8,128)(2,1)}, u32[]{:S(2)}) copy-start(bf16[1024,1152]{1,0:T(8,128)(2,1)} %fusion.63) | copy-start | bytes 7077892
  906.4 174.9 %reduce-scatter.12.cloned.1.call-start = ((), (), s32[]{:S(2)}) async-start(), calls=%async_computation.13 | async-start | bytes 15925248 | tf_op jit(solution)/shard_map/reduce_scatter | solution.py:362
  930.9 265.1 %reduce-scatter.6.cloned.1.call-start = ((), (), s32[]{:S(2)}) async-start(), calls=%async_computation.10 | async-start | bytes 17915904 | tf_op jit(solution)/shard_map/reduce_scatter | solution.py:346
  950.2 12.3 slice-start.14
  954.5 8.1 slice-start.15
  956.7 7.6 slice-start.4
  956.7 7.6 slice-start.5
  976.8 436.1 %all-reduce.6.cloned.1.call-start = ((), (), s32[]{:S(2)}) async-start(), calls=%async_computation.15 | async-start | bytes 11943936 | tf_op jit(solution)/shard_map/psum | solution.py:370
  (83 other events, 313.9 us)
Sparse Core Ops, SparseCore 0:
  11.1 89.1 all-gather.5
  102.8 52.4 all-gather.7
  157.7 30.1 all-gather.9
  190.2 78.6 all-gather.11
  271.2 48.7 all-gather.13
  469.0 43.0 reduce-scatter.9
  515.6 65.4 reduce-scatter.13
  906.5 69.2 reduce-scatter.7
  979.4 101.7 reduce-scatter.11
  1084.7 111.1 reduce-scatter.5
  1198.7 214.1 all-reduce.5
where the time goes:
time: 1440 us; the launch traced here: 1430 us
  matrix products  503 us (35%)
  waiting for transfers between devices  427 us (30%)
  local copies, waits for them, and re-layouts  167 us (12%)
  other arithmetic  146 us (10%)
  blocking collectives  107 us (7%)
  loops' own time  62.3 us (4%)
  between operations  16.7 us (1%)
    psum x1, waiting for transfers between devices, per_device(): lax.psum(grad_ada, 'rep').astype(jnp.float32)  120 us
    reduce_scatter x1, waiting for transfers between devices, per_device(): lax.psum_scatter(left_product(cond_act, grad_mod).astype(jnp.bfloat16), '...  115 us
    reduce_scatter x1, waiting for transfers between devices, per_device(): lax.psum_scatter(grad_gate_up.astype(jnp.bfloat16), 'fsdp', scatter_dimen...  104 us
    dot_general x5, matrix products, right_product(): lax.dot_general(left, right, (((1,), (1,)), ((), ())), preferred_element_...  92.2 us
    dot_general x16, matrix products, mask_scores(): jnp.einsum('hqd,hkd->hqk', query_b, keys_b, preferred_element_type=jnp.fl...  68.4 us
    dot_general x5, matrix products, left_product(): lax.dot_general(left, right, (((0,), (0,)), ((), ())), preferred_element_...  63.1 us
    dot_general x5, matrix products, product(): return jnp.dot(left, right, preferred_element_type=jnp.float32)  62.1 us
    dot_general x8, matrix products, one_block(): jnp.einsum('hqk,hqd->hkd', chance.astype(jnp.bfloat16), grad_result, pref...  55.7 us
  transfers between devices with their start and end apart: 11, of which 5 were waited for; matrix products, arithmetic and copies ran while one was open for 48% of the time, Pallas kernels for 0%

commit v1 on v0

v1 whole, which is shorter than its diff:
```python
import functools
import math

import jax
import jax.numpy as jnp
from jax import lax
from jax.experimental import pallas as pl
from jax.experimental.pallas import tpu as pltpu
from jax.sharding import PartitionSpec as P

D = 1152
HEADS = 16
HEAD_DIM = 72
SEQ_LEN = 1024
FF = 3072
ITEMS = 4
GRID = 16
epsilon = 1e-06
PAD = 24
FIRST = 256
BLK = 256
SCORE_EXP = HEAD_DIM ** (-0.5) * math.log2(math.e)
f32 = jnp.float32
bf16 = jnp.bfloat16


def dot_nn(a, b):
    return lax.dot_general(a, b, (((1,), (0,)), ((), ())), preferred_element_type=f32)


def dot_nt(a, b):
    return lax.dot_general(a, b, (((1,), (1,)), ((), ())), preferred_element_type=f32)


def block_at(index):
    return pl.ds(pl.multiple_of(index * BLK, BLK), BLK)


def turn(value, roll_ref, cos_t, up_t, down_t, sign):
    roll_ref[PAD : PAD + HEAD_DIM, :] = value
    above = roll_ref[PAD + 18 : PAD + 18 + HEAD_DIM, :]
    below = roll_ref[PAD - 18 : PAD - 18 + HEAD_DIM, :]
    return value * cos_t + sign * (above * up_t + below * down_t)


def normed(raw):
    factor = lax.rsqrt(jnp.sum(raw * raw, axis=0, keepdims=True) * (1.0 / HEAD_DIM) + epsilon)
    return raw * factor, factor


def fill_mask(seg_col_ref, seg_row_ref, mask_ref):
    for start in range(0, SEQ_LEN - FIRST, BLK):
        rows = seg_col_ref[FIRST + start : FIRST + start + BLK, :]
        cols = seg_row_ref[:, FIRST:]
        mask_ref[start : start + BLK, :] = jnp.where(rows == cols, 1.0, 0.0).astype(mask_ref.dtype)


def forward_kernel(q_ref, k_ref, v_ref, gq_ref, gk_ref, cos_ref, up_ref, down_ref, segc_ref, segr_ref,
                   o_ref, inv_ref, mask_ref, roll_ref, qt_ref, kk_ref, vt_ref):
    @pl.when(pl.program_id(0) == 0)
    def _():
        fill_mask(segc_ref, segr_ref, mask_ref)
        roll_ref[...] = jnp.zeros_like(roll_ref)

    for half in range(2):
        def prepare(index, carry):
            at = block_at(index)
            tables = (cos_ref[:, at], up_ref[:, at], down_ref[:, at])
            q_n, _ = normed(q_ref[half, :, at])
            qt_ref[half, :, at] = turn(q_n * gq_ref[...], roll_ref, *tables, 1.0).astype(bf16)
            k_n, _ = normed(k_ref[half, :, at])
            kk = turn(k_n * gk_ref[...], roll_ref, *tables, 1.0)
            kk_ref[half, at, :] = kk.T.astype(bf16)
            vt_ref[half, :, at] = v_ref[half, :, at].astype(bf16)
            return carry

        lax.fori_loop(0, SEQ_LEN // BLK, prepare, 0)

    def attend(at, lo, hi, mask):
        for half in range(2):
            scores = dot_nn(kk_ref[half, lo:hi, :], qt_ref[half, :, at])
            raised = jnp.exp2(scores * SCORE_EXP)
            if mask is not None:
                raised = raised * mask
            inverse = 1.0 / jnp.sum(raised, axis=0, keepdims=True)
            chance = (raised * inverse).astype(bf16)
            result = dot_nn(vt_ref[half, :, lo:hi], chance)
            o_ref[half * HEAD_DIM : (half + 1) * HEAD_DIM, at] = result.astype(bf16)
            inv_ref[half, :, at] = inverse

    attend(pl.ds(0, BLK), 0, FIRST, None)

    def later(index, carry):
        mask = mask_ref[:, block_at(index - 1)].astype(f32)
        attend(block_at(index), FIRST, SEQ_LEN, mask)
        return carry

    lax.fori_loop(1, SEQ_LEN // BLK, later, 0)


def backward_kernel(q_ref, k_ref, v_ref, g_ref, inv_ref, gq_ref, gk_ref, cos_ref, up_ref, down_ref, segc_ref,
                    segr_ref, d_ref, gain_ref, mask_ref, roll_ref, qt_ref, kt_ref, kk_ref, vv_ref,
                    dq_ref, dk_ref, dv_ref):
    @pl.when(pl.program_id(0) == 0)
    def _():
        fill_mask(segc_ref, segr_ref, mask_ref)
        roll_ref[...] = jnp.zeros_like(roll_ref)
        gain_ref[...] = jnp.zeros_like(gain_ref)

    for half in range(2):
        def prepare(index, carry):
            at = block_at(index)
            tables = (cos_ref[:, at], up_ref[:, at], down_ref[:, at])
            q_n, _ = normed(q_ref[half, :, at])
            qt_ref[half, :, at] = turn(q_n * gq_ref[...], roll_ref, *tables, 1.0).astype(bf16)
            k_n, _ = normed(k_ref[half, :, at])
            kk = turn(k_n * gk_ref[...], roll_ref, *tables, 1.0)
            kt_ref[half, :, at] = kk.astype(bf16)
            kk_ref[half, at, :] = kk.T.astype(bf16)
            vv_ref[half, at, :] = v_ref[half, :, at].T.astype(bf16)
            return carry

        lax.fori_loop(0, SEQ_LEN // BLK, prepare, 0)

    def attend(at, lo, hi, mask, first):
        for half in range(2):
            rows = slice(half * HEAD_DIM, (half + 1) * HEAD_DIM)
            q_b = qt_ref[half, :, at]
            g_b = g_ref[rows, at]
            scores = dot_nn(kk_ref[half, lo:hi, :], q_b)
            chance = jnp.exp2(scores * SCORE_EXP) * inv_ref[half, :, at]
            if mask is not None:
                chance = chance * mask
            grad_chance = dot_nn(vv_ref[half, lo:hi, :], g_b)
            delta = jnp.sum(chance * grad_chance, axis=0, keepdims=True)
            grad_scores = (chance * (grad_chance - delta)).astype(bf16)
            grad_v = dot_nt(g_b, chance.astype(bf16))
            grad_k = dot_nt(q_b, grad_scores)
            dq_ref[half, :, at] = dot_nn(kt_ref[half, :, lo:hi], grad_scores)
            if first:
                dv_ref[half, :, lo:hi] = grad_v
                dk_ref[half, :, lo:hi] = grad_k
            else:
                dv_ref[half, :, lo:hi] += grad_v
                dk_ref[half, :, lo:hi] += grad_k

    attend(pl.ds(0, BLK), 0, FIRST, None, True)
    dk_ref[:, :, FIRST:] = jnp.zeros((2, HEAD_DIM, SEQ_LEN - FIRST), f32)
    dv_ref[:, :, FIRST:] = jnp.zeros((2, HEAD_DIM, SEQ_LEN - FIRST), f32)

    def later(index, carry):
        mask = mask_ref[:, block_at(index - 1)].astype(f32)
        attend(block_at(index), FIRST, SEQ_LEN, mask, False)
        return carry

    lax.fori_loop(1, SEQ_LEN // BLK, later, 0)

    for half in range(2):
        rows = slice(half * HEAD_DIM, (half + 1) * HEAD_DIM)

        def finish(index, carry):
            at = block_at(index)
            tables = (cos_ref[:, at], up_ref[:, at], down_ref[:, at])
            for which, (raw_ref, grad_ref, weight_ref) in enumerate(((q_ref, dq_ref, gq_ref), (k_ref, dk_ref, gk_ref))):
                unit, factor = normed(raw_ref[half, :, at])
                grad = turn(grad_ref[half, :, at] * (HEAD_DIM ** -0.5), roll_ref, *tables, -1.0)
                part = grad * unit
                gain_ref[which] += part[:, :128] + part[:, 128:]
                grad = grad * weight_ref[...]
                mean = jnp.sum(grad * unit, axis=0, keepdims=True) * (1.0 / HEAD_DIM)
                d_ref[which, rows, at] = (factor * (grad - unit * mean)).astype(bf16)
            d_ref[2, rows, at] = dv_ref[half, :, at].astype(bf16)
            return carry

        lax.fori_loop(0, SEQ_LEN // BLK, finish, 0)


def whole(shape):
    return pl.BlockSpec(shape, lambda h: (0,) * len(shape))


def head_specs():
    return [pl.BlockSpec((2, HEAD_DIM, SEQ_LEN), lambda h, base=base: (base + h, 0, 0)) for base in (0, 8, 16)]


def table_specs():
    return [
        whole((HEAD_DIM, 1)), whole((HEAD_DIM, 1)),
        whole((HEAD_DIM, SEQ_LEN)), whole((HEAD_DIM, SEQ_LEN)), whole((HEAD_DIM, SEQ_LEN)),
        whole((SEQ_LEN, 1)), whole((1, SEQ_LEN)),
    ]


def work_scratch():
    return [
        pltpu.VMEM((SEQ_LEN - FIRST, SEQ_LEN - FIRST), bf16),
        pltpu.VMEM((HEAD_DIM + 2 * PAD, BLK), f32),
    ]


PAIR = (2, HEAD_DIM, SEQ_LEN)
TOKEN_PAIR = (2, SEQ_LEN, HEAD_DIM)


def attention_forward(raw, tables):
    return pl.pallas_call(
        forward_kernel,
        grid=(HEADS // 2,),
        in_specs=head_specs() + table_specs(),
        out_specs=[
            pl.BlockSpec((2 * HEAD_DIM, SEQ_LEN), lambda h: (h, 0)),
            pl.BlockSpec((2, 1, SEQ_LEN), lambda h: (h, 0, 0)),
        ],
        out_shape=[
            jax.ShapeDtypeStruct((D, SEQ_LEN), bf16),
            jax.ShapeDtypeStruct((HEADS, 1, SEQ_LEN), f32),
        ],
        scratch_shapes=work_scratch() + [
            pltpu.VMEM(PAIR, bf16), pltpu.VMEM(TOKEN_PAIR, bf16), pltpu.VMEM(PAIR, bf16),
        ],
        cost_estimate=pl.CostEstimate(flops=14_000_000_000, bytes_accessed=20_000_000, transcendentals=10_500_000),
        name="attend",
    )(raw, raw, raw, *tables)


def attention_backward(raw, grad_t, inverse, tables):
    return pl.pallas_call(
        backward_kernel,
        grid=(HEADS // 2,),
        in_specs=head_specs() + [
            pl.BlockSpec((2 * HEAD_DIM, SEQ_LEN), lambda h: (h, 0)),
            pl.BlockSpec((2, 1, SEQ_LEN), lambda h: (h, 0, 0)),
        ] + table_specs(),
        out_specs=[
            pl.BlockSpec((3, 2 * HEAD_DIM, SEQ_LEN), lambda h: (0, h, 0)),
            whole((2, HEAD_DIM, 128)),
        ],
        out_shape=[
            jax.ShapeDtypeStruct((3, D, SEQ_LEN), bf16),
            jax.ShapeDtypeStruct((2, HEAD_DIM, 128), f32),
        ],
        scratch_shapes=work_scratch() + [
            pltpu.VMEM(PAIR, bf16), pltpu.VMEM(PAIR, bf16), pltpu.VMEM(TOKEN_PAIR, bf16), pltpu.VMEM(TOKEN_PAIR, bf16),
            pltpu.VMEM(PAIR, f32), pltpu.VMEM(PAIR, f32), pltpu.VMEM(PAIR, f32),
        ],
        cost_estimate=pl.CostEstimate(flops=35_000_000_000, bytes_accessed=25_000_000, transcendentals=10_500_000),
        name="attend_back",
    )(raw, raw, raw, grad_t, inverse, *tables)


def product(left, right):
    return jnp.dot(left, right, preferred_element_type=f32)


def contract(left, right, left_dim, right_dim):
    return lax.dot_general(left, right, (((left_dim,), (right_dim,)), ((), ())), preferred_element_type=f32)


def angle_tables(heights, widths, lengths, segments):
    ends = jnp.cumsum(lengths)
    starts = ends - lengths
    places = jnp.arange(SEQ_LEN, dtype=jnp.int32)
    member = segments[:, None] == jnp.arange(ITEMS, dtype=jnp.int32)[None, :]
    start_tok = jnp.sum(jnp.where(member, starts[None, :], 0), axis=1)
    width_tok = jnp.sum(jnp.where(member, widths[None, :], 0), axis=1)
    height_tok = jnp.sum(jnp.where(member, heights[None, :], 0), axis=1)
    inside = width_tok > 0
    offset = places - start_tok
    safe_width = jnp.maximum(width_tok, 1)
    safe_height = jnp.maximum(height_tok, 1)
    row_index = jnp.where(inside, offset // safe_width, 0)
    col_index = jnp.where(inside, offset % safe_width, 0)
    height_f = safe_height.astype(f32)
    width_f = safe_width.astype(f32)
    row_place = jnp.where(inside, (row_index.astype(f32) - 0.5 * (height_f - 1.0)) * (GRID / height_f), 0.0)
    col_place = jnp.where(inside, (col_index.astype(f32) - 0.5 * (width_f - 1.0)) * (GRID / width_f), 0.0)
    quarter = HEAD_DIM // 4
    lane = jnp.arange(HEAD_DIM, dtype=jnp.int32)
    freqs = jnp.exp((lane % quarter).astype(f32) * (-math.log(10000.0) / quarter))
    place = jnp.where((lane < 2 * quarter)[:, None], row_place[None, :], col_place[None, :])
    angle = place * freqs[:, None]
    cos_t = jnp.cos(angle)
    sin_t = jnp.sin(angle)
    leading = (lane // quarter % 2 == 0)[:, None]
    return cos_t, jnp.where(leading, -sin_t, 0.0), jnp.where(leading, 0.0, sin_t)


def rms_scale(values):
    return lax.rsqrt(jnp.mean(values * values, axis=-1, keepdims=True) + epsilon)


def rms_back(grad_normed, normed_values, factor):
    return factor * (grad_normed - normed_values * jnp.mean(grad_normed * normed_values, axis=-1, keepdims=True))


def flip(array, axis, size, bit):
    return lax.ppermute(array, axis, [(i, i ^ bit) for i in range(size)])


def bits_of(size):
    return [1 << b for b in range(size.bit_length() - 1)]


def gather_steps(array, axis, size, dim):
    place = lax.axis_index(axis)
    for bit in bits_of(size):
        other = flip(array, axis, size, bit)
        low = (place & bit) == 0
        array = jnp.concatenate([jnp.where(low, array, other), jnp.where(low, other, array)], axis=dim)
    return array


def scatter_steps(array, axis, size):
    place = lax.axis_index(axis)
    for bit in bits_of(size):
        low = (place & bit) == 0
        pairs = array.reshape((array.shape[0] // 2, 2) + array.shape[1:])
        even, odd = pairs[:, 0], pairs[:, 1]
        received = flip(jnp.where(low, odd, even), axis, size, bit)
        array = jnp.where(low, even, odd) + received
    return array[0]


def butterfly_sum(array, axis, size):
    for bit in bits_of(size):
        array = array + flip(array, axis, size, bit)
    return array


def replica_sum(array, size, dim):
    place = lax.axis_index("rep")
    for bit in bits_of(size):
        low = (place & bit) == 0
        first, second = jnp.split(array, 2, axis=dim)
        received = flip(jnp.where(low, second, first), "rep", size, bit)
        array = (jnp.where(low, first, second).astype(f32) + received.astype(f32)).astype(bf16)
    for bit in reversed(bits_of(size)):
        low = (place & bit) == 0
        other = flip(array, "rep", size, bit)
        array = jnp.concatenate([jnp.where(low, array, other), jnp.where(low, other, array)], axis=dim)
    return array.astype(f32)


def per_device(
    fsdp,
    rep,
    tokens,
    condition,
    heights,
    widths,
    lengths,
    segments,
    ada_weight,
    ada_bias,
    qkv_weight,
    out_weight,
    gate_up_weight,
    down_weight,
    query_gain,
    key_gain,
    cotangent,
):
    place = lax.axis_index("fsdp")
    segment = segments[0]

    def gathered(weight):
        return lax.all_gather(weight.astype(bf16), "fsdp", axis=0, tiled=True)

    def scattered(grad):
        return lax.psum_scatter(grad.astype(bf16), "fsdp", scatter_dimension=0, tiled=True)

    qkv_full = gathered(qkv_weight)
    out_full = gathered(out_weight)
    gate_up_full = gathered(gate_up_weight)
    down_full = gathered(down_weight)

    shard = ada_weight.shape[0]
    cond_values = condition[0].astype(f32)
    cond_act = jax.nn.silu(cond_values).astype(bf16)
    cond_parts = cond_act.reshape(ITEMS, fsdp, shard).transpose(1, 0, 2)
    cond_cols = lax.all_to_all(cond_parts, "fsdp", 0, 0, tiled=True)
    ada_low = ada_weight.astype(bf16)
    partial = product(cond_cols.reshape(fsdp * ITEMS, shard), ada_low)
    bias_part = ada_bias.shape[0]
    bias_row = lax.dynamic_update_slice(
        jnp.zeros((6 * D,), f32), ada_bias.astype(bf16).astype(f32), (place * bias_part,)
    )
    modulation = scatter_steps((partial + bias_row[None, :]).reshape(fsdp, ITEMS, 6 * D), "fsdp", fsdp)

    segment_col = segment[:, None]

    def spread(which):
        rows = modulation[:, which * D : (which + 1) * D]
        result = jnp.zeros((SEQ_LEN, D), f32)
        for item in range(ITEMS):
            result = jnp.where(segment_col == item, rows[item][None, :], result)
        return result

    shift_a, scale_a, gate_a, shift_b, scale_b, gate_b = [spread(which) for which in range(6)]
    stream = tokens[0].astype(f32)
    factor_a = rms_scale(stream)
    normed_a = stream * factor_a
    hidden_a = (normed_a * (1.0 + scale_a) + shift_a).astype(bf16)
    raw = contract(qkv_full, hidden_a, 0, 1).reshape(3 * HEADS, HEAD_DIM, SEQ_LEN)
    tables = (
        query_gain[:, None],
        key_gain[:, None],
        *angle_tables(heights[0], widths[0], lengths[0], segment),
        segment_col,
        segment[None, :],
    )
    attended_t, inverse = attention_forward(raw, tables)
    branch_a = contract(attended_t, out_full, 0, 0)
    stream_b = stream + gate_a * branch_a
    factor_b = rms_scale(stream_b)
    normed_b = stream_b * factor_b
    hidden_b = (normed_b * (1.0 + scale_b) + shift_b).astype(bf16)
    gate_up = product(hidden_b, gate_up_full)
    gate_val = gate_up[:, :FF]
    up_val = gate_up[:, FF:]
    sigmoid_g = jax.nn.sigmoid(gate_val)
    inner = (gate_val * sigmoid_g * up_val).astype(bf16)
    branch_b = product(inner, down_full)
    result_tokens = (stream_b + gate_b * branch_b).astype(bf16)[None]

    upstream = cotangent[0].astype(f32)
    grad_gate_b = upstream * branch_b
    grad_branch_b = (upstream * gate_b).astype(bf16)
    grad_inner = contract(grad_branch_b, down_full, 1, 1)
    down_sum = scattered(contract(inner, grad_branch_b, 0, 0))
    grad_gate_val = grad_inner * up_val * sigmoid_g * (1.0 + gate_val * (1.0 - sigmoid_g))
    grad_up_val = grad_inner * gate_val * sigmoid_g
    grad_act = jnp.concatenate([grad_gate_val, grad_up_val], axis=1).astype(bf16)
    gate_up_sum = scattered(contract(hidden_b, grad_act, 0, 0))
    grad_hidden_b = contract(grad_act, gate_up_full, 1, 1)
    grad_scale_b = grad_hidden_b * normed_b
    grad_stream_b = upstream + rms_back(grad_hidden_b * (1.0 + scale_b), normed_b, factor_b)
    grad_gate_a = grad_stream_b * branch_a
    grad_branch_a = (grad_stream_b * gate_a).astype(bf16)
    out_sum = scattered(product(attended_t, grad_branch_a))
    grad_attended_t = contract(out_full, grad_branch_a, 1, 1).astype(bf16)
    grad_raw, gain_parts = attention_backward(raw, grad_attended_t, inverse, tables)
    grad_raw = grad_raw.reshape(3 * D, SEQ_LEN)
    qkv_sum = scattered(contract(hidden_a, grad_raw, 0, 1))
    grad_hidden_a = contract(grad_raw, qkv_full, 0, 1)
    stream_grad = grad_stream_b + rms_back(grad_hidden_a * (1.0 + scale_a), normed_a, factor_a)

    member = (segment[None, :] == jnp.arange(ITEMS, dtype=jnp.int32)[:, None]).astype(f32)

    def collect(piece):
        return jnp.dot(member, piece, precision=lax.Precision.HIGHEST).astype(bf16)

    def all_images(pieces):
        block = jnp.concatenate([collect(piece) for piece in pieces], axis=1)[None, None]
        return gather_steps(gather_steps(block, "rep", rep, 0), "fsdp", fsdp, 1)

    late_mod = all_images((grad_gate_a, grad_hidden_b, grad_scale_b, grad_gate_b))
    early_mod = all_images((grad_hidden_a, grad_hidden_a * normed_a))
    grad_mod = jnp.concatenate([early_mod, late_mod], axis=3)
    cond_all = gather_steps(cond_cols[None], "rep", rep, 0)
    images = rep * fsdp * ITEMS
    flat_mod = grad_mod.reshape(images, 6 * D)
    grad_ada = contract(cond_all.reshape(images, shard), flat_mod, 0, 0)
    bias_sum = jnp.sum(flat_mod.astype(f32), axis=0)
    grad_bias = lax.dynamic_slice(bias_sum, (place * bias_part,), (bias_part,))
    own_mod = lax.dynamic_index_in_dim(grad_mod, lax.axis_index("rep"), 0, keepdims=False)
    cond_back = contract(own_mod.reshape(fsdp * ITEMS, 6 * D), ada_low, 1, 1)
    cond_back = lax.all_to_all(cond_back.reshape(fsdp, ITEMS, shard), "fsdp", 0, 0, tiled=True)
    grad_cond_act = cond_back.transpose(1, 0, 2).reshape(ITEMS, D)
    sigmoid_c = jax.nn.sigmoid(cond_values)
    grad_condition = (grad_cond_act * sigmoid_c * (1.0 + cond_values * (1.0 - sigmoid_c))).astype(bf16)

    gains = jnp.sum(gain_parts, axis=2)
    gains = butterfly_sum(butterfly_sum(gains, "rep", rep), "fsdp", fsdp)
    return (
        result_tokens,
        stream_grad.astype(bf16)[None],
        grad_condition[None],
        grad_ada,
        grad_bias,
        replica_sum(qkv_sum, rep, 1),
        replica_sum(out_sum, rep, 1),
        replica_sum(gate_up_sum, rep, 1),
        replica_sum(down_sum, rep, 0),
        gains[0],
        gains[1],
    )


def solution(mesh):
    batch = ("fsdp", "rep")
    return jax.shard_map(
        functools.partial(per_device, mesh.shape["fsdp"], mesh.shape["rep"]),
        mesh=mesh,
        in_specs=(
            P(batch, None, None),
            P(batch, None, None),
            P(batch, None),
            P(batch, None),
            P(batch, None),
            P(batch, None),
            P("fsdp", None),
            P("fsdp"),
            P("fsdp", None),
            P("fsdp", None),
            P("fsdp", None),
            P("fsdp", None),
            P(),
            P(),
            P(batch, None, None),
        ),
        out_specs=(
            P(batch, None, None),
            P(batch, None, None),
            P(batch, None, None),
            P("fsdp", None),
            P("fsdp"),
            P("fsdp", None),
            P("fsdp", None),
            P("fsdp", None),
            P("fsdp", None),
            P(),
            P(),
        ),
        check_vma=False,
    )
```

time: 1440 us -> 791 us (0.55)
  matrix products: 503 us -> 234 us
  waiting for transfers between devices: 427 us -> 276 us
  local copies, waits for them, and re-layouts: 167 us -> 26.7 us
  Pallas kernels: 0 us -> 117 us
  blocking collectives: 107 us -> 0 us
  other arithmetic: 146 us -> 69.1 us
  loops' own time: 62.3 us -> 0 us
  starting transfers between devices: 0.46 us -> 41.8 us
    dot_general x83 -> x21, matrix products: 503 us -> 234 us  [the longest x11 164 us: contract(): lax.dot_general(left, right, (((left_dim,), (right_dim,)), ((), ())), pre...]
    reduce_scatter x5 -> x4, waiting for transfers between devices: 219 us -> 0.06 us  [scattered(): lax.psum_scatter(grad.astype(bf16), 'fsdp', scatter_dimension=0, tiled=True)]
    ppermute x0 -> x36, waiting for transfers between devices: none -> 216 us  [flip(): return lax.ppermute(array, axis, [(i, i ^ bit) for i in range(size)])]
    psum x1 -> x0, waiting for transfers between devices: 120 us -> none  [per_device(): lax.psum(grad_ada, 'rep').astype(jnp.float32)]
    pallas_call x0 -> x2, Pallas kernels: none -> 117 us  [the longest x1 68.7 us: attention_backward(): pl.pallas_call(backward_kernel, grid=(HEADS // 2,), in_specs=head_specs()...]
    another operation x6 -> x0, loops' own time: 62.3 us -> none  [the longest x1 29.8 us: per_device(): lax.map(attend, jnp.arange(seq_count * groups * blocks, dtype=jnp.int32))]
    psum x2 -> x0, blocking collectives: 56 us -> none  [the longest x1 41.7 us: per_device(): gains = lax.psum((query_gain_part, key_gain_part), ('fsdp', 'rep'))]
    unnamed x2 -> x0, blocking collectives: 51 us -> none
  transfers between devices with their start and end apart: 11 -> 46, of which waited for: 5 -> 30; matrix products, arithmetic and copies ran while one was open for 48% -> 30% of each run, Pallas kernels for 0% -> 15%
where the time goes in v1:
time: 791 us; the launch traced here: 781 us
  waiting for transfers between devices  276 us (35%)
  matrix products  234 us (30%)
  Pallas kernels  117 us (15%)
  other arithmetic  69.1 us (9%)
  starting transfers between devices  41.8 us (5%)
  local copies, waits for them, and re-layouts  26.7 us (3%)
  between operations  15.9 us (2%)
    ppermute x36, waiting for transfers between devices, flip(): return lax.ppermute(array, axis, [(i, i ^ bit) for i in range(size)])  216 us
    dot_general x11, matrix products, contract(): lax.dot_general(left, right, (((left_dim,), (right_dim,)), ((), ())), pre...  164 us
    pallas_call x1, Pallas kernels, attention_backward(): pl.pallas_call(backward_kernel, grid=(HEADS // 2,), in_specs=head_specs()...  68.7 us
    all_gather x4, waiting for transfers between devices, gathered(): return lax.all_gather(weight.astype(bf16), 'fsdp', axis=0, tiled=True)  59.5 us
    dot_general x4, matrix products, product(): return jnp.dot(left, right, preferred_element_type=f32)  53.2 us
    pallas_call x1, Pallas kernels, attention_forward(): pl.pallas_call(forward_kernel, grid=(HEADS // 2,), in_specs=head_specs()...  48.3 us
    ppermute x36, starting transfers between devices, flip(): return lax.ppermute(array, axis, [(i, i ^ bit) for i in range(size)])  32.7 us
    dot_general x6, matrix products, collect(): return jnp.dot(member, piece, precision=lax.Precision.HIGHEST).astype(bf16)  17.4 us
  transfers between devices with their start and end apart: 46, of which 30 were waited for; matrix products, arithmetic and copies ran while one was open for 30% of the time, Pallas kernels for 15%

profile of v1, /device:TPU:0, one launch (start us, length us, event | category | flops | bytes accessed | tf_op | source)
XLA Modules:
  0.0 780.8 jit_solution(10825734149481185602)
XLA Ops:
  14.2 5.2 all-to-all-start
  25.6 3.5 convolution_add_fusion
  35.7 6.5 collective-permute-done.1
  46.1 4.0 collective-permute-done.2
  50.6 17.4 %all-gather.5.cloned.1.call-done = bf16[1152,3456]{1,0:T(8,128)(2,1)} async-done(((bf16[144,3456]{1,0:T(8,128)(2,1)}), bf16[1152,3456]{1,0:T(8,128)(2,1)}) %all-gather.5.cloned.1.call-update) | async-done | bytes 7962640 | tf_op jit(solution)/shard_map/all_gather | solution.py:367
  68.0 18.3 %convolution_bitcast_fusion.1 = f32[3456,1024]{0,1:T(8,128)} fusion(bf16[1152,3456]{1,0:T(8,128)(2,1)} %all-gather.5.cloned.1.call-done, bf16[1,1024,1152]{2,1,0:T(8,128)(2,1)S(1)} %copy-done.2, f32[1152]{0:T(1024)S(1)} %get-tuple-element.31, f32[1152]{0:T(1024)S(1)} %get-tuple-element.32, f32[1152]{0:T(1024)S(1)} %get-tuple-element.33, ...), kind=kOutput, calls=%fused_computation.9 | convolution fusion | flops 8170242048 | bytes 24522752 | tf_op jit(solution)/shard_map/dot_general | solution.py:256
  86.5 15.2 %copy.111 = f32[3456,1024]{1,0:T(8,128)} copy(f32[3456,1024]{0,1:T(8,128)} %convolution_bitcast_fusion.1) | data formatting | bytes 28311552 | tf_op jit(solution)/shard_map/dot_general | solution.py:256
  101.7 48.3 %attend.1 = (bf16[1152,1024]{1,0:T(8,128)(2,1)}, f32[16,1,1024]{2,1,0:T(1,128)}) custom-call(f32[48,72,1024]{2,1,0:T(8,128)} %bitcast.185, f32[48,72,1024]{2,1,0:T(8,128)} %bitcast.186, f32[48,72,1024]{2,1,0:T(8,128)} %bitcast.187, f32[72,1]{1,0:T(8,128)} %copy.112.gq_ref, f32[72,1]{1,0:T(8,128)} %copy.113.gk_ref, f32[72,1024]{1,0:T(8,128)} %get-tuple-element.99.cos_ref, ...), custom_call_target="tpu_custom_call" | custom-call | flops 14000000000 | bytes 20000000 | tf_op jit(solution)/shard_map/attend/pallas_call | solution.py:206
  150.1 9.7 %multiply_reduce_fusion.1 = (f32[1024]{0:T(1024)S(1)}, f32[1024,1152]{1,0:T(8,128)}, f32[1024,1152]{1,0:T(8,128)}) fusion(f32[1152]{0:T(1024)S(1)} %get-tuple-element.40, pred[1024]{0:T(1024)(128)(4,1)S(1)} %get-tuple-element.103, f32[1152]{0:T(1024)S(1)} %get-tuple-element.41, pred[1024]{0:T(1024)(128)(4,1)S(1)} %get-tuple-element.104, ...), kind=kOutput, calls=%fused_computation.49 | convolution fusion | flops 2728524800 | bytes 16836608 | tf_op jit(solution)/shard_map/dot_general | solution.py:256
  159.8 22.1 %all-gather.9.cloned.1.call-done = bf16[1152,6144]{1,0:T(8,128)(2,1)} async-done(((bf16[144,6144]{1,0:T(8,128)(2,1)}), bf16[1152,6144]{1,0:T(8,128)(2,1)}) %all-gather.9.cloned.1.call-update) | async-done | bytes 14155792 | tf_op jit(solution)/shard_map/all_gather | solution.py:367
  182.0 31.0 %fusion.131 = f32[1024,6144]{1,0:T(8,128)} fusion(bf16[1152,6144]{1,0:T(8,128)(2,1)} %all-gather.9.cloned.1.call-done, f32[1024,1152]{1,0:T(8,128)} %get-tuple-element.51, f32[1152]{0:T(1024)S(1)} %get-tuple-element.20, f32[1152]{0:T(1024)S(1)} %get-tuple-element.21, f32[1152]{0:T(1024)S(1)} %get-tuple-element.22, f32[1152]{0:T(1024)S(1)} %get-tuple-element.23, ...), kind=kOutput, calls=%fused_computation.295 | convolution fusion | flops 14510850048 | bytes 44085248 | tf_op jit(solution)/shard_map/dot_general | solution.py:252
  212.9 20.0 %all-gather.11.cloned.1.call-done = bf16[3072,1152]{1,0:T(8,128)(2,1)} async-done(((bf16[384,1152]{1,0:T(8,128)(2,1)}), bf16[3072,1152]{1,0:T(8,128)(2,1)}) %all-gather.11.cloned.1.call-update) | async-done | bytes 7077904 | tf_op jit(solution)/shard_map/all_gather | solution.py:367
  232.9 22.1 %multiply_convert_fusion.1 = (bf16[1024,3072]{1,0:T(8,128)(2,1)}, bf16[1024,3072]{1,0:T(8,128)(2,1)}, bf16[1024,3072]{1,0:T(8,128)(2,1)}) fusion(f32[1024,6144]{1,0:T(8,128)} %fusion.131, bf16[3072,1152]{1,0:T(8,128)(2,1)} %all-gather.11.cloned.1.call-done, bf16[1,1024,1152]{2,1,0:T(8,128)(2,1)S(1)} %copy-done.4, f32[1152]{0:T(1024)S(1)} %get-tuple-element.28, ...), kind=kOutput, calls=%fused_computation.4 | convolution fusion | flops 7306346496 | bytes 53499904 | tf_op jit(solution)/shard_map/dot_general | solution.py:256
  255.0 14.2 %fusion.133 = f32[1024,1152]{1,0:T(8,128)} fusion(bf16[1024,3072]{1,0:T(8,128)(2,1)} %get-tuple-element.54, bf16[3072,1152]{1,0:T(8,128)(2,1)} %all-gather.11.cloned.1.call-done), kind=kOutput, calls=%fused_computation.296 | convolution fusion | flops 7247757312 | bytes 18087936 | tf_op jit(solution)/shard_map/dot_general | solution.py:252
  269.2 24.1 %fusion = f32[1024,1152]{1,0:T(8,128)} fusion(bf16[1152,6144]{1,0:T(8,128)(2,1)} %all-gather.9.cloned.1.call-done, bf16[1024,3072]{1,0:T(8,128)(2,1)} %get-tuple-element.53, bf16[1024,3072]{1,0:T(8,128)(2,1)} %get-tuple-element.52), kind=kOutput, calls=%fused_computation.10 | convolution fusion | flops 14520680448 | bytes 31457280 | tf_op jit(solution)/shard_map/dot_general | solution.py:256
  293.3 8.1 %multiply_reduce_fusion = (f32[1024]{0:T(1024)S(1)}, bf16[1,1024,1152]{2,1,0:T(8,128)(2,1)}) fusion(f32[1024,1152]{1,0:T(8,128)} %get-tuple-element.51, f32[1024,1152]{1,0:T(8,128)} %fusion, f32[1152]{0:T(1024)S(1)} %get-tuple-element.24, f32[1152]{0:T(1024)S(1)} %get-tuple-element.25, f32[1152]{0:T(1024)S(1)} %get-tuple-element.26, ...), kind=kLoop, calls=%fused_computation.44 | loop fusion | flops 18873344 | bytes 16564224 | tf_op jit(solution)/shard_map/reduce_sum | solution.py:293
  301.5 13.1 %multiply_convert_fusion.3 = (bf16[1024,1152]{1,0:T(8,128)(2,1)S(1)}, f32[1024,1152]{1,0:T(8,128)}) fusion(f32[1152]{0:T(1024)S(1)} %copy-done.26, f32[1152]{0:T(1024)S(1)} %copy-done.28, f32[1152]{0:T(1024)S(1)} %copy-done.30, f32[1152]{0:T(1024)S(1)} %copy-done.24, pred[1024]{0:T(1024)(128)(4,1)S(1)} %get-tuple-element.103, ...), kind=kLoop, calls=%fused_computation.43 | loop fusion | flops 21233664 | bytes 18923520 | tf_op jit(solution)/shard_map/convert_element_type | solution.py:439
  316.0 4.6 convolution_convert_fusion.3
  320.7 13.5 %convolution_convert_fusion.2 = bf16[3072,1152]{1,0:T(8,128)(2,1)} fusion(bf16[1024,3072]{1,0:T(8,128)(2,1)} %get-tuple-element.54, bf16[1,1024,1152]{2,1,0:T(8,128)(2,1)S(1)} %copy-done.4, f32[1152]{0:T(1024)S(1)} %get-tuple-element.28, f32[1152]{0:T(1024)S(1)} %get-tuple-element.29, f32[1152]{0:T(1024)S(1)} %get-tuple-element.30, ...), kind=kOutput, calls=%fused_computation.7 | convolution fusion | flops 7259553792 | bytes 15751168 | tf_op jit(solution)/shard_map/dot_general | solution.py:256
  335.9 6.2 fusion.30.g_ref
  342.2 68.7 %attend_back.1 = (bf16[3,1152,1024]{2,1,0:T(8,128)(2,1)}, f32[2,72,128]{2,1,0:T(8,128)}) custom-call(f32[48,72,1024]{2,1,0:T(8,128)} %bitcast.188, f32[48,72,1024]{2,1,0:T(8,128)} %bitcast.189, f32[48,72,1024]{2,1,0:T(8,128)} %bitcast.190, bf16[1152,1024]{1,0:T(8,128)(2,1)} %fusion.30.g_ref, f32[16,1,1024]{2,1,0:T(1,128)} %get-tuple-element.16.inv_ref, ...), custom_call_target="tpu_custom_call" | custom-call | flops 35000000512 | bytes 25000000 | tf_op jit(solution)/shard_map/attend_back/pallas_call | solution.py:227
  411.0 17.4 %convolution_convert_fusion.1 = bf16[1152,3456]{1,0:T(8,128)(2,1)} fusion(bf16[3456,1024]{1,0:T(8,128)(2,1)} %bitcast.208, bf16[1,1024,1152]{2,1,0:T(8,128)(2,1)S(1)} %copy-done.3, f32[1152]{0:T(1024)S(1)} %copy-done.46, f32[1152]{0:T(1024)S(1)} %copy-done.48, f32[1152]{0:T(1024)S(1)} %copy-done.50, f32[1152]{0:T(1024)S(1)} %copy-done.52, ...), kind=kOutput, calls=%fused_computation.1 | convolution fusion | flops 8174223360 | bytes 17444864 | tf_op jit(solution)/shard_map/dot_general | solution.py:256
  439.3 18.0 %fusion.10 = (f32[1024]{0:T(1024)S(1)}, f32[1024,1152]{1,0:T(8,128)S(1)}) fusion(bf16[1,1024,1152]{2,1,0:T(8,128)(2,1)S(1)} %copy-done.3, f32[1152]{0:T(1024)S(1)} %copy-done.32, f32[1152]{0:T(1024)S(1)} %copy-done.34, f32[1152]{0:T(1024)S(1)} %copy-done.36, f32[1152]{0:T(1024)S(1)} %copy-done.22, f32[1024]{0:T(1024)S(1)} %copy-done.18, ...), kind=kOutput, calls=%fused_computation.27 | convolution fusion | flops 8165522432 | bytes 22149120 | tf_op jit(solution)/shard_map/dot_general | solution.py:256
  465.4 28.8 %convolution_convert_fusion = bf16[1152,6144]{1,0:T(8,128)(2,1)} fusion(bf16[1024,3072]{1,0:T(8,128)(2,1)} %get-tuple-element.53, bf16[1024,3072]{1,0:T(8,128)(2,1)} %get-tuple-element.52, f32[1024,1152]{1,0:T(8,128)} %get-tuple-element.51, f32[1152]{0:T(1024)S(1)} %copy-done.38, f32[1152]{0:T(1024)S(1)} %copy-done.40, f32[1152]{0:T(1024)S(1)} %copy-done.42, ...), kind=kOutput, calls=%fused_computation | convolution fusion | flops 14543093760 | bytes 31502336 | tf_op jit(solution)/shard_map/dot_general | solution.py:256
  494.1 5.6 fusion.72
  502.5 4.2 fusion.78
  513.2 11.8 %fusion.68 = bf16[1,1024,1152]{2,1,0:T(8,128)(2,1)} fusion(f32[1024,1152]{1,0:T(8,128)} %get-tuple-element.49, f32[1024]{0:T(1024)S(1)} %broadcast_multiply_fusion, bf16[1,1024,1152]{2,1,0:T(8,128)(2,1)S(1)} %copy-done.3, f32[1024,1152]{1,0:T(8,128)} %copy-done.1, f32[1152]{0:T(1024)S(1)} %copy-done.32, pred[1024]{0:T(1024)(128)(4,1)S(1)} %get-tuple-element.103, ...), kind=kLoop, calls=%fused_computation.93 | loop fusion | flops 15335424 | bytes 14186496 | tf_op jit(solution)/shard_map/broadcast_in_dim | solution.py:477
  525.8 3.0 collective-permute-start.9
  535.7 4.2 collective-permute-done.6
  541.1 7.7 collective-permute-done.11
  549.6 6.6 collective-permute-done.7
  556.6 23.4 %collective-permute-done.12 = bf16[4,4,4,4608]{3,2,1,0:T(4,128)(2,1)S(1)} collective-permute-done((bf16[4,4,4,4608]{3,2,1,0:T(4,128)(2,1)S(1)}, bf16[4,4,4,4608]{3,2,1,0:T(4,128)(2,1)S(1)}, u32[]{:S(2)}, u32[]{:S(2)}) %collective-permute-start.12) | collective-permute-done | bytes 589856 | tf_op jit(solution)/shard_map/ppermute | solution.py:297
  583.4 2.8 fusion.79
  586.9 3.6 all-to-all-start.1
  595.7 3.9 collective-permute-done.20
  604.5 3.2 collective-permute-done.21
  607.9 9.1 %collective-permute-done.27 = bf16[192,1152]{1,0:T(8,128)(2,1)S(1)} collective-permute-done((bf16[192,1152]{1,0:T(8,128)(2,1)S(1)}, bf16[192,1152]{1,0:T(8,128)(2,1)S(1)}, u32[]{:S(2)}, u32[]{:S(2)}) %collective-permute-start.27) | collective-permute-done | bytes 442400 | tf_op jit(solution)/shard_map/ppermute | solution.py:297
  620.2 9.1 %collective-permute-done.28 = bf16[96,1152]{1,0:T(8,128)(2,1)S(1)} collective-permute-done((bf16[96,1152]{1,0:T(8,128)(2,1)S(1)}, bf16[96,1152]{1,0:T(8,128)(2,1)S(1)}, u32[]{:S(2)}, u32[]{:S(2)}) %collective-permute-start.28) | collective-permute-done | bytes 221216 | tf_op jit(solution)/shard_map/ppermute | solution.py:297
  630.4 11.1 %collective-permute-done.29 = bf16[96,1152]{1,0:T(8,128)(2,1)S(1)} collective-permute-done((bf16[96,1152]{1,0:T(8,128)(2,1)S(1)}, bf16[96,1152]{1,0:T(8,128)(2,1)S(1)}, u32[]{:S(2)}, u32[]{:S(2)}) %collective-permute-start.29) | collective-permute-done | bytes 221216 | tf_op jit(solution)/shard_map/ppermute | solution.py:297
  647.0 7.7 collective-permute-done.30
  654.9 10.9 %collective-permute-done.15 = bf16[144,1728]{1,0:T(8,128)(2,1)S(1)} collective-permute-done((bf16[144,1728]{1,0:T(8,128)(2,1)S(1)}, bf16[144,1728]{1,0:T(8,128)(2,1)S(1)}, u32[]{:S(2)}, u32[]{:S(2)}) %collective-permute-start.15) | collective-permute-done | bytes 497696 | tf_op jit(solution)/shard_map/ppermute | solution.py:297
  667.0 22.4 %collective-permute-done.23 = bf16[144,3072]{1,0:T(8,128)(2,1)S(1)} collective-permute-done((bf16[144,3072]{1,0:T(8,128)(2,1)S(1)}, bf16[144,3072]{1,0:T(8,128)(2,1)S(1)}, u32[]{:S(2)}, u32[]{:S(2)}) %collective-permute-start.23) | collective-permute-done | bytes 884768 | tf_op jit(solution)/shard_map/ppermute | solution.py:297
  691.6 2.8 collective-permute-start.17
  694.4 22.1 %collective-permute-done.24 = bf16[144,1536]{1,0:T(8,128)(2,1)S(1)} collective-permute-done((bf16[144,1536]{1,0:T(8,128)(2,1)S(1)}, bf16[144,1536]{1,0:T(8,128)(2,1)S(1)}, u32[]{:S(2)}, u32[]{:S(2)}) %collective-permute-start.24) | collective-permute-done | bytes 442400 | tf_op jit(solution)/shard_map/ppermute | solution.py:297
  716.8 14.8 %collective-permute-done.17 = bf16[144,864]{1,0:T(8,128)(2,1)S(1)} collective-permute-done((bf16[144,864]{1,0:T(8,128)(2,1)S(1)}, bf16[144,864]{1,0:T(8,128)(2,1)S(1)}, u32[]{:S(2)}, u32[]{:S(2)}) %collective-permute-start.17) | collective-permute-done | bytes 248864 | tf_op jit(solution)/shard_map/ppermute | solution.py:297
  731.9 9.2 %collective-permute-done.25 = bf16[144,1536]{1,0:T(8,128)(2,1)S(1)} collective-permute-done((bf16[144,1536]{1,0:T(8,128)(2,1)S(1)}, bf16[144,1536]{1,0:T(8,128)(2,1)S(1)}, u32[]{:S(2)}, u32[]{:S(2)}) %collective-permute-start.25) | collective-permute-done | bytes 442400 | tf_op jit(solution)/shard_map/ppermute | solution.py:297
  741.3 10.8 %collective-permute-done.18 = bf16[144,1728]{1,0:T(8,128)(2,1)S(1)} collective-permute-done((bf16[144,1728]{1,0:T(8,128)(2,1)S(1)}, bf16[144,1728]{1,0:T(8,128)(2,1)S(1)}, u32[]{:S(2)}, u32[]{:S(2)}) %collective-permute-start.18) | collective-permute-done | bytes 497696 | tf_op jit(solution)/shard_map/ppermute | solution.py:297
  753.9 17.1 %collective-permute-done.26 = bf16[144,3072]{1,0:T(8,128)(2,1)S(1)} collective-permute-done((bf16[144,3072]{1,0:T(8,128)(2,1)S(1)}, bf16[144,3072]{1,0:T(8,128)(2,1)S(1)}, u32[]{:S(2)}, u32[]{:S(2)}) %collective-permute-start.26) | collective-permute-done | bytes 884768 | tf_op jit(solution)/shard_map/ppermute | solution.py:297
  (308 shorter events, 97.8 us)
Async XLA Ops:
  7.2 60.9 %all-gather.5.cloned.1.call-start = ((), (), s32[]{:S(2)}) async-start(), calls=%async_computation.6 | async-start | bytes 8957952 | tf_op jit(solution)/shard_map/all_gather | solution.py:367
  10.0 140.0 %all-gather.7.cloned.1.call-start = ((), (), s32[]{:S(2)}) async-start(), calls=%async_computation.7 | async-start | bytes 2985984 | tf_op jit(solution)/shard_map/all_gather | solution.py:367
  12.0 170.0 %all-gather.9.cloned.1.call-start = ((), (), s32[]{:S(2)}) async-start(), calls=%async_computation.8 | async-start | bytes 15925248 | tf_op jit(solution)/shard_map/all_gather | solution.py:367
  14.2 10.8 %all-to-all-start = ((bf16[8,4,144]{2,1,0:T(4,128)(2,1)}), bf16[8,4,144]{2,1,0:T(4,128)(2,1)S(1)}, u32[]{:S(2)}, u32[]{:S(2)}) async-start(bf16[8,4,144]{2,1,0:T(4,128)(2,1)} %copy.102), calls=%async_computation | async-start | bytes 32768 | tf_op jit(solution)/shard_map/all_to_all | solution.py:381
  19.4 213.5 %all-gather.11.cloned.1.call-start = ((), (), s32[]{:S(2)}) async-start(), calls=%async_computation.9 | async-start | bytes 7962624 | tf_op jit(solution)/shard_map/all_gather | solution.py:367
  22.2 559.9 %reduce-scatter.7.cloned.1.call-start = ((), (), s32[]{:S(2)}) async-start(), calls=%async_computation.11 | async-start | bytes 2985984 | tf_op jit(solution)/shard_map/reduce_scatter | solution.py:370
  30.6 3.1 collective-permute-start
  34.0 8.2 %collective-permute-start.1 = (f32[2,4,6912]{2,1,0:T(4,128)S(1)}, f32[2,4,6912]{2,1,0:T(4,128)S(1)}, u32[]{:S(2)}, u32[]{:S(2)}) collective-permute-start(f32[2,4,6912]{2,1,0:T(4,128)S(1)} %select_bitcast_fusion.1), channel_id=1, source_target_pairs={{0,8},{4,12},{8,0},{12,4},{16,24},{20,28},{24,16},{28,20},{1,9},{5... | collective-permute-start | bytes 663560 | tf_op jit(solution)/shard_map/ppermute | solution.py:297
  42.4 7.7 collective-permute-start.2
  50.6 131.4 %copy-start.37 = (f32[1152]{0:T(1024)}, f32[1152]{0:T(1024)S(1)}, u32[]{:S(2)}) copy-start(f32[1152]{0:T(1024)S(1)} %get-tuple-element.20) | copy-start | bytes 13828
  50.6 131.4 %copy-start.39 = (f32[1152]{0:T(1024)}, f32[1152]{0:T(1024)S(1)}, u32[]{:S(2)}) copy-start(f32[1152]{0:T(1024)S(1)} %get-tuple-element.21) | copy-start | bytes 13828
  320.7 279.1 %reduce-scatter.11.cloned.1.call-start = ((), (), s32[]{:S(2)}) async-start(), calls=%async_computation.13 | async-start | bytes 7962624 | tf_op jit(solution)/shard_map/reduce_scatter | solution.py:370
  334.2 307.5 %reduce-scatter.5.cloned.1.call-start = ((), (), s32[]{:S(2)}) async-start(), calls=%async_computation.10 | async-start | bytes 8957952 | tf_op jit(solution)/shard_map/reduce_scatter | solution.py:370
  428.3 216.9 %reduce-scatter.9.cloned.1.call-start = ((), (), s32[]{:S(2)}) async-start(), calls=%async_computation.12 | async-start | bytes 15925248 | tf_op jit(solution)/shard_map/reduce_scatter | solution.py:370
  429.0 3.7 collective-permute-start.13
  432.8 4.9 collective-permute-start.14
  437.8 62.0 %collective-permute-start.31 = (f32[2,72]{1,0:T(2,128)S(1)}, f32[2,72]{1,0:T(2,128)S(1)}, u32[]{:S(2)}, u32[]{:S(2)}) collective-permute-start(f32[2,72]{1,0:T(2,128)S(1)} %reduce_sum.89), channel_id=1, source_target_pairs={{0,1},{1,0},{2,3},{3,2},{4,5},{5,4},{6,7},{7,6},{8,9},{9,8},{10,11... | collective-permute-start | bytes 1736 | tf_op jit(solution)/shard_map/ppermute | solution.py:297
  461.2 64.3 %collective-permute-start.3 = (bf16[1,1,4,2304]{3,2,1,0:T(4,128)(2,1)S(1)}, bf16[1,1,4,2304]{3,2,1,0:T(4,128)(2,1)S(1)}, u32[]{:S(2)}, u32[]{:S(2)}) collective-permute-start(bf16[1,1,4,2304]{3,2,1,0:T(4,128)(2,1)S(1)} %maximum_bitcast_fusion.1), channel_id=1, source_target_pairs={{0,1},{1,0},{2,3},{3,2},{4,5},{5,4},{6,7},{7,6},{8,9},{9,8},{10,11... | collective-permute-start | bytes 55304 | tf_op jit(solution)/shard_map/ppermute | solution.py:297
  499.8 7.0 collective-permute-start.32
  506.7 1.9 collective-permute-start.33
  506.9 18.8 %collective-permute-start.8 = (bf16[1,1,4,4608]{3,2,1,0:T(4,128)(2,1)S(1)}, bf16[1,1,4,4608]{3,2,1,0:T(4,128)(2,1)S(1)}, u32[]{:S(2)}, u32[]{:S(2)}) collective-permute-start(bf16[1,1,4,4608]{3,2,1,0:T(4,128)(2,1)S(1)} %maximum_bitcast_fusion), channel_id=1, source_target_pairs={{0,1},{1,0},{2,3},{3,2},{4,5},{5,4},{6,7},{7,6},{8,9},{9,8},{10,11... | collective-permute-start | bytes 110600 | tf_op jit(solution)/shard_map/ppermute | solution.py:297
  508.7 3.6 collective-permute-start.34
  512.3 12.7 %collective-permute-start.35 = (f32[2,72]{1,0:T(2,128)S(1)}, f32[2,72]{1,0:T(2,128)S(1)}, u32[]{:S(2)}, u32[]{:S(2)}) collective-permute-start(f32[2,72]{1,0:T(2,128)S(1)} %add.234), channel_id=1, source_target_pairs={{0,16},{4,20},{8,24},{12,28},{16,0},{20,4},{24,8},{28,12},{1,17},{... | collective-permute-start | bytes 1736 | tf_op jit(solution)/shard_map/ppermute | solution.py:297
  525.6 5.9 collective-permute-start.4
  525.8 6.5 collective-permute-start.9
  531.6 1.3 collective-permute-start.5
  532.5 1.4 collective-permute-start.10
  533.2 6.8 collective-permute-start.6
  534.3 14.5 %collective-permute-start.11 = (bf16[4,2,4,4608]{3,2,1,0:T(4,128)(2,1)S(1)}, bf16[4,2,4,4608]{3,2,1,0:T(4,128)(2,1)S(1)}, u32[]{:S(2)}, u32[]{:S(2)}) collective-permute-start(bf16[4,2,4,4608]{3,2,1,0:T(4,128)(2,1)S(1)} %pad_maximum_fusion.8), channel_id=1, source_target_pairs={{0,8},{4,12},{8,0},{12,4},{16,24},{20,28},{24,16},{28,20},{1,9},{5... | collective-permute-start | bytes 884744 | tf_op jit(solution)/shard_map/ppermute | solution.py:297
  540.3 15.9 %collective-permute-start.7 = (bf16[4,4,4,2304]{3,2,1,0:T(4,128)(2,1)S(1)}, bf16[4,4,4,2304]{3,2,1,0:T(4,128)(2,1)S(1)}, u32[]{:S(2)}, u32[]{:S(2)}) collective-permute-start(bf16[4,4,4,2304]{3,2,1,0:T(4,128)(2,1)S(1)} %pad_maximum_fusion.7), channel_id=1, source_target_pairs={{0,16},{4,20},{8,24},{12,28},{16,0},{20,4},{24,8},{28,12},{1,17},{... | collective-permute-start | bytes 884744 | tf_op jit(solution)/shard_map/ppermute | solution.py:297
  549.6 30.4 %collective-permute-start.12 = (bf16[4,4,4,4608]{3,2,1,0:T(4,128)(2,1)S(1)}, bf16[4,4,4,4608]{3,2,1,0:T(4,128)(2,1)S(1)}, u32[]{:S(2)}, u32[]{:S(2)}) collective-permute-start(bf16[4,4,4,4608]{3,2,1,0:T(4,128)(2,1)S(1)} %pad_maximum_fusion.4), channel_id=1, source_target_pairs={{0,16},{4,20},{8,24},{12,28},{16,0},{20,4},{24,8},{28,12},{1,17},{... | collective-permute-start | bytes 1769480 | tf_op jit(solution)/shard_map/ppermute | solution.py:297
  583.3 7.2 collective-permute-start.19
  586.9 8.7 %all-to-all-start.1 = ((f32[8,4,144]{2,1,0:T(4,128)}), f32[8,4,144]{2,1,0:T(4,128)S(1)}, u32[]{:S(2)}, u32[]{:S(2)}) async-start(f32[8,4,144]{2,1,0:T(4,128)} %copy.120), calls=%async_computation.1 | async-start | bytes 65536 | tf_op jit(solution)/shard_map/all_to_all | solution.py:468
  590.8 8.7 %collective-permute-start.20 = (bf16[144,288]{1,0:T(8,128)(2,1)S(1)}, bf16[144,288]{1,0:T(8,128)(2,1)S(1)}, u32[]{:S(2)}, u32[]{:S(2)}) collective-permute-start(bf16[144,288]{1,0:T(8,128)(2,1)S(1)} %broadcast_select_fusion.33), channel_id=1, source_target_pairs={{0,2},{1,3},{2,0},{3,1},{4,6},{5,7},{6,4},{7,5},{8,10},{9,11},{10,... | collective-permute-start | bytes 248840 | tf_op jit(solution)/shard_map/ppermute | solution.py:297
  599.7 8.0 %collective-permute-start.21 = (bf16[144,288]{1,0:T(8,128)(2,1)S(1)}, bf16[144,288]{1,0:T(8,128)(2,1)S(1)}, u32[]{:S(2)}, u32[]{:S(2)}) collective-permute-start(bf16[144,288]{1,0:T(8,128)(2,1)S(1)} %add_convert_fusion.9), channel_id=1, source_target_pairs={{0,2},{1,3},{2,0},{3,1},{4,6},{5,7},{6,4},{7,5},{8,10},{9,11},{10,... | collective-permute-start | bytes 248840 | tf_op jit(solution)/shard_map/ppermute | solution.py:297
  601.0 16.0 %collective-permute-start.27 = (bf16[192,1152]{1,0:T(8,128)(2,1)S(1)}, bf16[192,1152]{1,0:T(8,128)(2,1)S(1)}, u32[]{:S(2)}, u32[]{:S(2)}) collective-permute-start(bf16[192,1152]{1,0:T(8,128)(2,1)S(1)} %broadcast_select_fusion.10), channel_id=1, source_target_pairs={{0,1},{1,0},{2,3},{3,2},{4,5},{5,4},{6,7},{7,6},{8,9},{9,8},{10,11... | collective-permute-start | bytes 1327112 | tf_op jit(solution)/shard_map/ppermute | solution.py:297
  607.8 12.3 %collective-permute-start.22 = (bf16[144,576]{1,0:T(8,128)(2,1)S(1)}, bf16[144,576]{1,0:T(8,128)(2,1)S(1)}, u32[]{:S(2)}, u32[]{:S(2)}) collective-permute-start(bf16[144,576]{1,0:T(8,128)(2,1)S(1)} %pad_maximum_fusion.9), channel_id=1, source_target_pairs={{0,1},{1,0},{2,3},{3,2},{4,5},{5,4},{6,7},{7,6},{8,9},{9,8},{10,11... | collective-permute-start | bytes 497672 | tf_op jit(solution)/shard_map/ppermute | solution.py:297
  618.4 10.9 %collective-permute-start.28 = (bf16[96,1152]{1,0:T(8,128)(2,1)S(1)}, bf16[96,1152]{1,0:T(8,128)(2,1)S(1)}, u32[]{:S(2)}, u32[]{:S(2)}) collective-permute-start(bf16[96,1152]{1,0:T(8,128)(2,1)S(1)} %broadcast_select_fusion.23), channel_id=1, source_target_pairs={{0,2},{1,3},{2,0},{3,1},{4,6},{5,7},{6,4},{7,5},{8,10},{9,11},{10,... | collective-permute-start | bytes 663560 | tf_op jit(solution)/shard_map/ppermute | solution.py:297
  629.3 12.2 %collective-permute-start.29 = (bf16[96,1152]{1,0:T(8,128)(2,1)S(1)}, bf16[96,1152]{1,0:T(8,128)(2,1)S(1)}, u32[]{:S(2)}, u32[]{:S(2)}) collective-permute-start(bf16[96,1152]{1,0:T(8,128)(2,1)S(1)} %add_convert_fusion.7), channel_id=1, source_target_pairs={{0,2},{1,3},{2,0},{3,1},{4,6},{5,7},{6,4},{7,5},{8,10},{9,11},{10,... | collective-permute-start | bytes 663560 | tf_op jit(solution)/shard_map/ppermute | solution.py:297
  641.6 13.1 %collective-permute-start.30 = (bf16[192,1152]{1,0:T(8,128)(2,1)S(1)}, bf16[192,1152]{1,0:T(8,128)(2,1)S(1)}, u32[]{:S(2)}, u32[]{:S(2)}) collective-permute-start(bf16[192,1152]{1,0:T(8,128)(2,1)S(1)} %pad_maximum_fusion.6), channel_id=1, source_target_pairs={{0,1},{1,0},{2,3},{3,2},{4,5},{5,4},{6,7},{7,6},{8,9},{9,8},{10,11... | collective-permute-start | bytes 1327112 | tf_op jit(solution)/shard_map/ppermute | solution.py:297
  643.2 22.6 %collective-permute-start.15 = (bf16[144,1728]{1,0:T(8,128)(2,1)S(1)}, bf16[144,1728]{1,0:T(8,128)(2,1)S(1)}, u32[]{:S(2)}, u32[]{:S(2)}) collective-permute-start(bf16[144,1728]{1,0:T(8,128)(2,1)S(1)} %broadcast_select_fusion.7), channel_id=1, source_target_pairs={{0,1},{1,0},{2,3},{3,2},{4,5},{5,4},{6,7},{7,6},{8,9},{9,8},{10,11... | collective-permute-start | bytes 1493000 | tf_op jit(solution)/shard_map/ppermute | solution.py:297
  646.9 42.4 %collective-permute-start.23 = (bf16[144,3072]{1,0:T(8,128)(2,1)S(1)}, bf16[144,3072]{1,0:T(8,128)(2,1)S(1)}, u32[]{:S(2)}, u32[]{:S(2)}) collective-permute-start(bf16[144,3072]{1,0:T(8,128)(2,1)S(1)} %broadcast_select_fusion.2), channel_id=1, source_target_pairs={{0,1},{1,0},{2,3},{3,2},{4,5},{5,4},{6,7},{7,6},{8,9},{9,8},{10,11... | collective-permute-start | bytes 2654216 | tf_op jit(solution)/shard_map/ppermute | solution.py:297
  666.3 25.1 %collective-permute-start.16 = (bf16[144,864]{1,0:T(8,128)(2,1)S(1)}, bf16[144,864]{1,0:T(8,128)(2,1)S(1)}, u32[]{:S(2)}, u32[]{:S(2)}) collective-permute-start(bf16[144,864]{1,0:T(8,128)(2,1)S(1)} %broadcast_select_fusion.20), channel_id=1, source_target_pairs={{0,2},{1,3},{2,0},{3,1},{4,6},{5,7},{6,4},{7,5},{8,10},{9,11},{10,... | collective-permute-start | bytes 746504 | tf_op jit(solution)/shard_map/ppermute | solution.py:297
  689.8 26.7 %collective-permute-start.24 = (bf16[144,1536]{1,0:T(8,128)(2,1)S(1)}, bf16[144,1536]{1,0:T(8,128)(2,1)S(1)}, u32[]{:S(2)}, u32[]{:S(2)}) collective-permute-start(bf16[144,1536]{1,0:T(8,128)(2,1)S(1)} %broadcast_select_fusion.13), channel_id=1, source_target_pairs={{0,2},{1,3},{2,0},{3,1},{4,6},{5,7},{6,4},{7,5},{8,10},{9,11},{10,... | collective-permute-start | bytes 1327112 | tf_op jit(solution)/shard_map/ppermute | solution.py:297
  691.6 40.0 %collective-permute-start.17 = (bf16[144,864]{1,0:T(8,128)(2,1)S(1)}, bf16[144,864]{1,0:T(8,128)(2,1)S(1)}, u32[]{:S(2)}, u32[]{:S(2)}) collective-permute-start(bf16[144,864]{1,0:T(8,128)(2,1)S(1)} %add_convert_fusion.6), channel_id=1, source_target_pairs={{0,2},{1,3},{2,0},{3,1},{4,6},{5,7},{6,4},{7,5},{8,10},{9,11},{10,... | collective-permute-start | bytes 746504 | tf_op jit(solution)/shard_map/ppermute | solution.py:297
  716.7 24.3 %collective-permute-start.25 = (bf16[144,1536]{1,0:T(8,128)(2,1)S(1)}, bf16[144,1536]{1,0:T(8,128)(2,1)S(1)}, u32[]{:S(2)}, u32[]{:S(2)}) collective-permute-start(bf16[144,1536]{1,0:T(8,128)(2,1)S(1)} %add_convert_fusion.5), channel_id=1, source_target_pairs={{0,2},{1,3},{2,0},{3,1},{4,6},{5,7},{6,4},{7,5},{8,10},{9,11},{10,... | collective-permute-start | bytes 1327112 | tf_op jit(solution)/shard_map/ppermute | solution.py:297
  731.8 20.3 %collective-permute-start.18 = (bf16[144,1728]{1,0:T(8,128)(2,1)S(1)}, bf16[144,1728]{1,0:T(8,128)(2,1)S(1)}, u32[]{:S(2)}, u32[]{:S(2)}) collective-permute-start(bf16[144,1728]{1,0:T(8,128)(2,1)S(1)} %pad_maximum_fusion.5), channel_id=1, source_target_pairs={{0,1},{1,0},{2,3},{3,2},{4,5},{5,4},{6,7},{7,6},{8,9},{9,8},{10,11... | collective-permute-start | bytes 1493000 | tf_op jit(solution)/shard_map/ppermute | solution.py:297
  741.2 29.7 %collective-permute-start.26 = (bf16[144,3072]{1,0:T(8,128)(2,1)S(1)}, bf16[144,3072]{1,0:T(8,128)(2,1)S(1)}, u32[]{:S(2)}, u32[]{:S(2)}) collective-permute-start(bf16[144,3072]{1,0:T(8,128)(2,1)S(1)} %pad_maximum_fusion.3), channel_id=1, source_target_pairs={{0,1},{1,0},{2,3},{3,2},{4,5},{5,4},{6,7},{7,6},{8,9},{9,8},{10,11... | collective-permute-start | bytes 2654216 | tf_op jit(solution)/shard_map/ppermute | solution.py:297
  (59 other events, 2066.4 us)
Sparse Core Ops, SparseCore 0:
  10.5 57.5 all-gather.4
  70.5 30.1 all-gather.6
  103.1 78.7 all-gather.8
  184.3 48.6 all-gather.10
  320.8 42.9 reduce-scatter.6
  367.2 65.4 reduce-scatter.10
  436.2 69.2 reduce-scatter.4
  510.3 117.2 reduce-scatter.8
